TPU v7x, 128 devices: a whole 4x4x4 slice. The times are simulated.
128 devices in a mesh: seg: 4 (over y), expert: 32 (over x, z, core).
Axes of the slice: x: 4, y: 4, z: 4, core: 2. Of those that a mesh axis runs over, the one named last changes fastest.
Arguments:
- frames: bfloat16 [32768, 1536], P(('seg', 'expert')), may hold values from -6 to 6
- expert_ids: int32 [32768, 2], P(('seg', 'expert')), may hold values from 0 to 31, all different within a row; in each aligned block of 256 rows (0 to 255, 256 to 511, ...) at most 24 rows name the same one
- gate_weights: float32 [32768, 2], P(('seg', 'expert')), may hold values from 0.2 to 1
- up_weight: bfloat16 [32, 1536, 2048], P('expert'), may hold values from -0.15625 to 0.15625
- down_weight: bfloat16 [32, 2048, 1536], P('expert'), may hold values from -0.125 to 0.125
- out_weight: bfloat16 [1536, 64], replicated, may hold values from -0.15625 to 0.15625
- in_conv: bfloat16 [7, 64, 2048], replicated, may hold values from -0.25 to 0.25
- snake_first: float32 [2048], replicated, may hold values from 0.5 to 2
- first_up: bfloat16 [16, 2048, 512], P(None, None, 'seg'), may hold values from -0.09375 to 0.09375
Outputs:
- features: float32 [4, 65536, 512], P(None, 'expert', 'seg')
Inputs may be any that keep to these rules, and one draw needn't show every extreme that they name: `expert_ids`: in each aligned block of 256 rows (the rows of one device) no expert is named by more than 24 of the block's choices, and some block reaches 24; the two ids of a token differ.
All inputs are finite; a program needn't handle non-finite values.
Results may differ from a plain program's by a relative error of at most 0.005.
Values may be sent and summed in bfloat16 or wider, within the bound.
A program may use at most 128 MiB of HBM per device.

v0:
```python
import jax
import jax.numpy as jnp
from jax import lax
from jax.sharding import PartitionSpec as P


def with_halo(value, sides, width):
    for axis, dim in sides:
        size, length = (lax.axis_size(axis), value.shape[dim])
        up = [(i, (i + 1) % size) for i in range(size - 1)]
        down = [(j, i) for i, j in up]
        last = lax.slice_in_dim(value, length - width, length, axis=dim)
        leading = lax.slice_in_dim(value, 0, width, axis=dim)
        before = lax.ppermute(last, axis, up)
        after = lax.ppermute(leading, axis, down)
        value = jnp.concatenate([before, value, after], axis=dim)
    return value


def snake_act(values, alpha_row):
    return values + jnp.sin(alpha_row * values) ** 2 / alpha_row


def slot_dest(expert_ids, num_experts, capacity):
    flat_ids = expert_ids.reshape(-1)
    one_hot = (flat_ids[:, None] == jnp.arange(num_experts, dtype=jnp.int32)[None, :]).astype(
        jnp.int32
    )
    before = jnp.cumsum(one_hot, axis=0) - one_hot
    return flat_ids * capacity + jnp.sum(before * one_hot, axis=1)


def conv_seven(padded, weights, length):
    windows = [
        lax.slice_in_dim(padded, tap_index, tap_index + length, axis=1) for tap_index in range(7)
    ]
    stacked = jnp.concatenate(windows, axis=2)
    return jnp.einsum(
        "klc,co->klo",
        stacked,
        weights.reshape(-1, weights.shape[2]),
        preferred_element_type=jnp.float32,
    )


def upsample(padded, weights, length):
    prev_rows = padded[:, 0:length]
    here_rows = padded[:, 1 : length + 1]
    next_rows = padded[:, 2 : length + 2]
    middle = jnp.einsum(
        "klc,rco->klro", here_rows, weights[4:12], preferred_element_type=jnp.float32
    )
    early_part = jnp.einsum(
        "klc,rco->klro", prev_rows, weights[12:16], preferred_element_type=jnp.float32
    )
    later_part = jnp.einsum(
        "klc,rco->klro", next_rows, weights[0:4], preferred_element_type=jnp.float32
    )
    joined = middle + jnp.concatenate([early_part, later_part], axis=2)
    return joined.reshape(padded.shape[0], length * 8, weights.shape[2])


def local(
    frames,
    expert_ids,
    gate_weights,
    up_weight,
    down_weight,
    out_weight,
    in_conv,
    snake_first,
    first_up,
):
    tok_rows, model_dim = frames.shape
    num_experts = lax.axis_size("expert")
    capacity = 3 * tok_rows // num_experts
    dest_slot = slot_dest(expert_ids, num_experts, capacity)
    source_rows = jnp.repeat(frames, 2, axis=0)
    send_buffer = (
        jnp.zeros((num_experts * capacity, model_dim), jnp.bfloat16).at[dest_slot].set(source_rows)
    )
    send_buffer = send_buffer.reshape(num_experts, capacity, model_dim)
    upper_weight = up_weight[0]
    lower_weight = down_weight[0]
    received = lax.all_to_all(send_buffer, "expert", split_axis=0, concat_axis=0, tiled=True)
    count_src, count_rows, _ = received.shape
    flat_rows = received.reshape(count_src * count_rows, model_dim)
    hidden_units = jax.nn.gelu(
        jnp.dot(flat_rows, upper_weight, preferred_element_type=jnp.float32), approximate=True
    ).astype(jnp.bfloat16)
    expert_out = jnp.dot(hidden_units, lower_weight, preferred_element_type=jnp.float32).astype(
        jnp.bfloat16
    )
    processed = expert_out.reshape(count_src, count_rows, expert_out.shape[1])
    returned = lax.all_to_all(processed, "expert", split_axis=0, concat_axis=0, tiled=True)
    picked_rows = returned.reshape(num_experts * capacity, model_dim)[dest_slot]
    picked = jnp.dot(picked_rows, out_weight, preferred_element_type=jnp.float32)
    lat_dim = out_weight.shape[1]
    gated = jnp.sum(picked.reshape(tok_rows, 2, lat_dim) * gate_weights[:, :, None], axis=1)
    latent = jnp.dot(frames, out_weight, preferred_element_type=jnp.float32) + gated
    latent_low = latent.astype(jnp.bfloat16)
    lat_padded = with_halo(latent_low, (("expert", 0),), 3)
    first_in = conv_seven(lat_padded[None], in_conv, tok_rows)[0]
    act_first = snake_act(first_in, snake_first).astype(jnp.bfloat16)
    pad_first = with_halo(act_first, (("expert", 0),), 1)
    return upsample(lax.all_gather(pad_first[None], "seg", axis=0, tiled=True), first_up, tok_rows)


def solution(mesh):
    placed = (
        P(("seg", "expert"), None),
        P(("seg", "expert"), None),
        P(("seg", "expert"), None),
        P("expert", None, None),
        P("expert", None, None),
        P(),
        P(),
        P(),
        P(None, None, "seg"),
    )
    return jax.shard_map(
        local, mesh=mesh, in_specs=placed, out_specs=P(None, "expert", "seg"), check_vma=False
    )
```

profile of v0, /device:TPU:1, one launch (start us, length us, event | category | flops | bytes accessed | tf_op | source)
XLA Modules:
  0.0 225.3 jit_solution(10748287871956991975)
XLA Ops:
  6.5 0.8 broadcast_multiply_fusion
  7.4 0.8 copy.19
  8.2 0.1 eq.29
  8.3 0.1 eq.25
  8.5 0.1 copy.18
  8.6 0.1 mul.58
  8.8 1.2 reduce-window.6
  9.9 0.2 slice_reduce_fusion
  10.2 2.0 broadcast_in_dim.9
  12.2 1.5 reshape.99
  13.8 5.5 %scatter_custom_fusion = bf16[768,1536]{1,0:T(8,128)(2,1)} fusion(s32[512]{0:T(512)S(1)} %bitcast.91, bf16[512,1536]{1,0:T(8,128)(2,1)} %reshape.99, bf16[]{:T(256)} %constant.9.clone.1), kind=kCustom, calls=%fused_computation.35 | custom fusion | bytes 2359808 | tf_op jit(solution)/shard_map/scatter | solution.py:80
  19.3 41.0 %all_to_all.10 = bf16[32,24,1536]{2,1,0:T(8,128)(2,1)} all-to-all(bf16[32,24,1536]{2,1,0:T(8,128)(2,1)} %bitcast.87), channel_id=1, replica_groups=mesh['seg'=4,'expert'=32] {'expert'}, dimensions={0} | all-to-all | bytes 4718592 | tf_op jit(solution)/shard_map/all_to_all | solution.py:85
  60.3 16.6 %fusion.17 = bf16[768,1536]{1,0:T(8,128)(2,1)} fusion(bf16[1,2048,1536]{2,1,0:T(8,128)(2,1)} %param.13, bf16[768,1536]{1,0:T(8,128)(2,1)} %bitcast.89, bf16[1,1536,2048]{2,1,0:T(8,128)(2,1)} %param.12), kind=kOutput, calls=%fused_computation.25 | convolution fusion | flops 9679011840 | bytes 17301504 | tf_op jit(solution)/shard_map/dot_general | solution.py:91
  76.9 4.7 %all-to-all-start.1 = ((bf16[32,24,1536]{2,1,0:T(8,128)(2,1)}), bf16[32,24,1536]{2,1,0:T(8,128)(2,1)}, u32[]{:S(2)}, u32[]{:S(2)}) async-start(bf16[32,24,1536]{2,1,0:T(8,128)(2,1)} %bitcast.88), calls=%async_computation.1 | async-start | bytes 4718592 | tf_op jit(solution)/shard_map/all_to_all | solution.py:95
  81.9 31.1 %all-to-all-done.1 = bf16[32,24,1536]{2,1,0:T(8,128)(2,1)} async-done(((bf16[32,24,1536]{2,1,0:T(8,128)(2,1)}), bf16[32,24,1536]{2,1,0:T(8,128)(2,1)}, u32[]{:S(2)}, u32[]{:S(2)}) %all-to-all-start.1) | async-done | bytes 2359328 | tf_op jit(solution)/shard_map/all_to_all | solution.py:95
  112.9 5.6 %gather_fusion = bf16[512,1536]{1,0:T(8,128)(2,1)S(1)} fusion(bf16[768,1536]{1,0:T(8,128)(2,1)} %bitcast.8, s32[1024]{0:T(1024)S(1)} %pad_clamp_fusion), kind=kCustom, calls=%fused_computation | custom fusion | bytes 3147776 | tf_op jit(solution)/shard_map/gather | solution.py:96
  118.5 1.5 fusion.52
  120.0 0.4 multiply_reduce_fusion
  120.5 1.5 fusion.37
  122.1 2.4 %collective-permute-start = (bf16[3,64]{0,1:T(8,128)(2,1)S(1)}, bf16[3,64]{0,1:T(8,128)(2,1)S(1)}, u32[]{:S(2)}, u32[]{:S(2)}) collective-permute-start(bf16[3,64]{0,1:T(8,128)(2,1)S(1)} %get-tuple-element.7), channel_id=1, source_target_pairs={{0,1},{1,2},{2,3},{3,4},{4,5},{5,6},{6,7},{7,8},{8,9},{9,10},{10,1... | collective-permute-start | bytes 1160 | tf_op jit(solution)/shard_map/ppermute | solution.py:14
  124.5 2.2 collective-permute-start.1
  126.7 2.9 %collective-permute-done.1 = bf16[3,64]{0,1:T(8,128)(2,1)S(1)} collective-permute-done((bf16[3,64]{0,1:T(8,128)(2,1)S(1)}, bf16[3,64]{0,1:T(8,128)(2,1)S(1)}, u32[]{:S(2)}, u32[]{:S(2)}) %collective-permute-start.1) | collective-permute-done | bytes 416 | tf_op jit(solution)/shard_map/ppermute | solution.py:15
  130.2 8.7 %add_convert_fusion = bf16[256,2048]{1,0:T(8,128)(2,1)S(1)} fusion(f32[2048]{0:T(1024)S(1)} %copy-done.3, bf16[448,2048]{1,0:T(8,128)(2,1)S(1)} %bitcast.86, bf16[1,256,448]{1,2,0:T(8,128)(2,1)S(1)} %slice_dynamic-update-slice_fusion), kind=kOutput, calls=%fused_computation.34 | convolution fusion | flops 472383488 | bytes 3121152 | tf_op jit(solution)/shard_map/klc,co->klo/dot_general | solution.py:38
  138.9 1.9 collective-permute-start.2
  140.9 2.4 %collective-permute-start.3 = (bf16[1,2048]{1,0:T(2,128)(2,1)S(1)}, bf16[1,2048]{1,0:T(2,128)(2,1)S(1)}, u32[]{:S(2)}, u32[]{:S(2)}) collective-permute-start(bf16[1,2048]{1,0:T(2,128)(2,1)S(1)} %get-tuple-element.6), channel_id=1, source_target_pairs={{1,0},{2,1},{3,2},{4,3},{5,4},{6,5},{7,6},{8,7},{9,8},{10,9},{11,1... | collective-permute-start | bytes 12296 | tf_op jit(solution)/shard_map/ppermute | solution.py:15
  143.3 2.6 %collective-permute-done.3 = bf16[1,2048]{1,0:T(2,128)(2,1)S(1)} collective-permute-done((bf16[1,2048]{1,0:T(2,128)(2,1)S(1)}, bf16[1,2048]{1,0:T(2,128)(2,1)S(1)}, u32[]{:S(2)}, u32[]{:S(2)}) %collective-permute-start.3) | collective-permute-done | bytes 4128 | tf_op jit(solution)/shard_map/ppermute | solution.py:15
  145.8 1.3 maximum_bitcast_fusion
  147.2 52.8 %all-gather.4.cloned.1.call-done = bf16[4,258,2048]{2,1,0:T(8,128)(2,1)} async-done(((bf16[1,258,2048]{2,1,0:T(8,128)(2,1)}), bf16[4,258,2048]{2,1,0:T(8,128)(2,1)}) %all-gather.4.cloned.1.call-update) | async-done | bytes 4227088 | tf_op jit(solution)/shard_map/all_gather | solution.py:106
  200.0 5.3 %fusion.13 = f32[4,256,4,128]{3,1,2,0:T(8,128)S(1)} fusion(bf16[4,258,2048]{2,1,0:T(8,128)(2,1)} %all-gather.4.cloned.1.call-done, bf16[16,2048,128]{2,1,0:T(8,128)(2,1)} %param.17), kind=kOutput, calls=%fused_computation.18 | convolution fusion | flops 2147483648 | bytes 8388608 | tf_op jit(solution)/shard_map/klc,rco->klro/dot_general | solution.py:53
  205.3 4.1 %fusion.12 = f32[4,256,4,128]{3,1,2,0:T(8,128)S(1)} fusion(bf16[4,258,2048]{2,1,0:T(8,128)(2,1)S(1)} %copy-done.2, bf16[16,2048,128]{2,1,0:T(8,128)(2,1)} %param.17), kind=kOutput, calls=%fused_computation.16 | convolution fusion | flops 2147483648 | bytes 8388608 | tf_op jit(solution)/shard_map/klc,rco->klro/dot_general | solution.py:56
  209.5 4.5 %maximum_add_fusion = f32[4,256,8,128]{3,1,2,0:T(8,128)S(1)} fusion(f32[4,256,4,128]{3,1,2,0:T(8,128)S(1)} %fusion.12, f32[4,256,4,128]{3,1,2,0:T(8,128)S(1)} %fusion.13, bf16[16,2048,128]{2,1,0:T(8,128)(2,1)S(1)} %bitcast.95, bf16[4,258,2048]{2,1,0:T(8,128)(2,1)S(1)} %copy-done.2), kind=kOutput, calls=%fused_computation.21 | convolution fusion | flops 4297064448 | bytes 16777216 | tf_op jit(solution)/shard_map/klc,rco->klro/dot_general | solution.py:50
  214.0 4.4 %copy.33 = f32[4,256,8,128]{3,2,1,0:T(8,128)} copy(f32[4,256,8,128]{3,1,2,0:T(8,128)S(1)} %maximum_add_fusion) | data formatting | bytes 8388608 | tf_op jit(solution)/shard_map/add | solution.py:59
  (35 shorter events, 1.1 us)
Async XLA Ops:
  6.5 123.6 %copy-start = (bf16[7,64,2048]{2,1,0:T(8,128)(2,1)S(1)}, bf16[7,64,2048]{2,1,0:T(8,128)(2,1)}, u32[]{:S(2)}) copy-start(bf16[7,64,2048]{2,1,0:T(8,128)(2,1)} %param.15) | copy-start | bytes 5505028
  76.9 4.8 %copy-start.1 = (f32[256,2]{0,1:T(2,128)S(1)}, f32[256,2]{0,1:T(2,128)}, u32[]{:S(2)}) copy-start(f32[256,2]{0,1:T(2,128)} %param.11) | copy-start | bytes 6148
  76.9 36.0 %all-to-all-start.1 = ((bf16[32,24,1536]{2,1,0:T(8,128)(2,1)}), bf16[32,24,1536]{2,1,0:T(8,128)(2,1)}, u32[]{:S(2)}, u32[]{:S(2)}) async-start(bf16[32,24,1536]{2,1,0:T(8,128)(2,1)} %bitcast.88), calls=%async_computation.1 | async-start | bytes 4718592 | tf_op jit(solution)/shard_map/all_to_all | solution.py:95
  81.6 118.3 %all-gather.4.cloned.1.call-start = ((), (), s32[]{:S(2)}) async-start(), calls=%async_computation.2 | async-start | bytes 5406720 | tf_op jit(solution)/shard_map/all_gather | solution.py:106
  118.5 11.6 %copy-start.3 = (f32[2048]{0:T(1024)S(1)}, f32[2048]{0:T(1024)}, u32[]{:S(2)}) copy-start(f32[2048]{0:T(1024)} %param.16) | copy-start | bytes 24580
  122.1 4.6 %collective-permute-start = (bf16[3,64]{0,1:T(8,128)(2,1)S(1)}, bf16[3,64]{0,1:T(8,128)(2,1)S(1)}, u32[]{:S(2)}, u32[]{:S(2)}) collective-permute-start(bf16[3,64]{0,1:T(8,128)(2,1)S(1)} %get-tuple-element.7), channel_id=1, source_target_pairs={{0,1},{1,2},{2,3},{3,4},{4,5},{5,6},{6,7},{7,8},{8,9},{9,10},{10,1... | collective-permute-start | bytes 1160 | tf_op jit(solution)/shard_map/ppermute | solution.py:14
  124.5 5.1 %collective-permute-start.1 = (bf16[3,64]{0,1:T(8,128)(2,1)S(1)}, bf16[3,64]{0,1:T(8,128)(2,1)S(1)}, u32[]{:S(2)}, u32[]{:S(2)}) collective-permute-start(bf16[3,64]{0,1:T(8,128)(2,1)S(1)} %get-tuple-element.8), channel_id=1, source_target_pairs={{1,0},{2,1},{3,2},{4,3},{5,4},{6,5},{7,6},{8,7},{9,8},{10,9},{11,1... | collective-permute-start | bytes 1160 | tf_op jit(solution)/shard_map/ppermute | solution.py:15
  138.9 4.3 %collective-permute-start.2 = (bf16[1,2048]{1,0:T(2,128)(2,1)S(1)}, bf16[1,2048]{1,0:T(2,128)(2,1)S(1)}, u32[]{:S(2)}, u32[]{:S(2)}) collective-permute-start(bf16[1,2048]{1,0:T(2,128)(2,1)S(1)} %get-tuple-element.5), channel_id=1, source_target_pairs={{0,1},{1,2},{2,3},{3,4},{4,5},{5,6},{6,7},{7,8},{8,9},{9,10},{10,1... | collective-permute-start | bytes 12296 | tf_op jit(solution)/shard_map/ppermute | solution.py:14
  140.9 5.0 %collective-permute-start.3 = (bf16[1,2048]{1,0:T(2,128)(2,1)S(1)}, bf16[1,2048]{1,0:T(2,128)(2,1)S(1)}, u32[]{:S(2)}, u32[]{:S(2)}) collective-permute-start(bf16[1,2048]{1,0:T(2,128)(2,1)S(1)} %get-tuple-element.6), channel_id=1, source_target_pairs={{1,0},{2,1},{3,2},{4,3},{5,4},{6,5},{7,6},{8,7},{9,8},{10,9},{11,1... | collective-permute-start | bytes 12296 | tf_op jit(solution)/shard_map/ppermute | solution.py:15
  200.0 5.3 %copy-start.2 = (bf16[4,258,2048]{2,1,0:T(8,128)(2,1)S(1)}, bf16[4,258,2048]{2,1,0:T(8,128)(2,1)}, u32[]{:S(2)}) copy-start(bf16[4,258,2048]{2,1,0:T(8,128)(2,1)} %all-gather.4.cloned.1.call-done) | copy-start | bytes 12681220
  200.0 9.4 %slice-start = ((s8[8388608]{0:T(1024)(128)(4,1)}), s8[4194304]{0:T(1024)(128)(4,1)S(1)}, s32[]{:S(2)}) async-start(s8[8388608]{0:T(1024)(128)(4,1)} %bitcast.94), calls=%async_computation.3 | async-start | bytes 8388608
  205.3 4.1 %slice-start.1 = ((s8[8388608]{0:T(1024)(128)(4,1)}), s8[4194304]{0:T(1024)(128)(4,1)S(1)}, s32[]{:S(2)}) async-start(s8[8388608]{0:T(1024)(128)(4,1)} %bitcast.94), calls=%async_computation.4 | async-start | bytes 8388608
Sparse Core Ops, SparseCore 0:
  147.3 52.6 all-gather.3
where the time goes:
time: 226 us; the launch traced here: 225 us
  waiting for transfers between devices  89.4 us (40%)
  matrix products  42.3 us (19%)
  blocking collectives  41 us (18%)
  local copies, waits for them, and re-layouts  21.4 us (9%)
  between operations  13.7 us (6%)
  starting transfers between devices  13.6 us (6%)
  other arithmetic  3.95 us (2%)
    all_gather x1, waiting for transfers between devices, local(): lax.all_gather(pad_first[None], 'seg', axis=0, tiled=True)  52.8 us
    all_to_all x1, blocking collectives, local(): lax.all_to_all(send_buffer, 'expert', split_axis=0, concat_axis=0, tiled=...  41 us
    all_to_all x1, waiting for transfers between devices, local(): lax.all_to_all(processed, 'expert', split_axis=0, concat_axis=0, tiled=True)  31.1 us
    dot_general x1, matrix products, local(): jnp.dot(hidden_units, lower_weight, preferred_element_type=jnp.float32)  16.6 us
    dot_general x1, matrix products, conv_seven(): jnp.einsum('klc,co->klo', stacked, weights.reshape(-1, weights.shape[2]),...  8.72 us
    gather x1, local copies, waits for them, and re-layouts, local(): picked_rows = returned.reshape(num_experts * capacity, model_dim)[dest_slot]  5.57 us
    scatter x1, local copies, waits for them, and re-layouts, local(): jnp.zeros((num_experts * capacity, model_dim), jnp.bfloat16).at[dest_slot]  5.52 us
    ppermute x2, waiting for transfers between devices, with_halo(): after = lax.ppermute(leading, axis, down)  5.43 us
  transfers between devices with their start and end apart: 6, of which 4 were waited for; matrix products, arithmetic and copies ran while one was open for 0% of the time, Pallas kernels for 0%

commit v1 on v0

v1 whole, which is shorter than its diff:
```python
import jax
import jax.numpy as jnp
from jax import lax
from jax.sharding import PartitionSpec as P

SIN2 = (
    9.869604110717773,
    -32.469669342041016,
    42.727195739746094,
    -30.101465225219727,
    13.05009937286377,
    -3.3565926551818848,
)
PI_INV = 0.3183098861837907


def snake_act(values, freq, inv_alpha):
    turns = values * freq
    frac = turns - jnp.round(turns)
    t = frac * frac
    q = jnp.float32(SIN2[5])
    for coef in SIN2[4::-1]:
        q = q * t + coef
    return values + jnp.minimum(q * t, 1.0) * inv_alpha


def edge_rows(value, width):
    size = lax.axis_size("expert")
    up = [(i, (i + 1) % size) for i in range(size - 1)]
    down = [(j, i) for i, j in up]
    before = lax.ppermute(value[-width:], "expert", up)
    after = lax.ppermute(value[:width], "expert", down)
    return jnp.concatenate([before, value, after], axis=0)


def conv_seven(padded, weights, length):
    windows = [lax.slice_in_dim(padded, tap, tap + length, axis=1) for tap in range(7)]
    stacked = jnp.concatenate(windows, axis=2)
    return jnp.einsum(
        "klc,co->klo",
        stacked,
        weights.reshape(-1, weights.shape[2]),
        preferred_element_type=jnp.float32,
    )


def upsample(padded, weights, length):
    prev_rows = padded[:, 0:length]
    here_rows = padded[:, 1 : length + 1]
    next_rows = padded[:, 2 : length + 2]
    middle = jnp.einsum(
        "klc,rco->klro", here_rows, weights[4:12], preferred_element_type=jnp.float32
    )
    early_part = jnp.einsum(
        "klc,rco->klro", prev_rows, weights[12:16], preferred_element_type=jnp.float32
    )
    later_part = jnp.einsum(
        "klc,rco->klro", next_rows, weights[0:4], preferred_element_type=jnp.float32
    )
    joined = middle + jnp.concatenate([early_part, later_part], axis=2)
    return joined.reshape(padded.shape[0], length * 8, weights.shape[2])


def local(
    frames,
    expert_ids,
    gate_weights,
    up_weight,
    down_weight,
    out_weight,
    in_conv,
    snake_first,
    first_up,
):
    tok_rows, model_dim = frames.shape
    num_experts = lax.axis_size("expert")
    capacity = 3 * tok_rows // num_experts
    lat_dim = out_weight.shape[1]

    experts = jnp.arange(num_experts, dtype=jnp.int32)[:, None]
    first = expert_ids[:, 0][None, :] == experts
    second = expert_ids[:, 1][None, :] == experts
    named = first | second
    row = jnp.arange(tok_rows, dtype=jnp.int32)
    earlier = (row[:, None] < row[None, :]).astype(jnp.bfloat16)
    rank = jnp.dot(named.astype(jnp.bfloat16), earlier, preferred_element_type=jnp.float32)
    slots = jnp.arange(capacity, dtype=jnp.int32).astype(jnp.float32)
    pick = (rank[:, None, :] == slots[None, :, None]) & named[:, None, :]
    gates = jnp.where(first, gate_weights[:, 0][None, :], 0.0) + jnp.where(
        second, gate_weights[:, 1][None, :], 0.0
    )
    weighted = jnp.where(pick, gates[:, None, :], 0.0).reshape(-1, tok_rows)

    send = jnp.dot(
        pick.reshape(-1, tok_rows).astype(jnp.bfloat16), frames, preferred_element_type=jnp.float32
    ).astype(jnp.bfloat16)
    send = send.reshape(num_experts, capacity, model_dim)
    received = lax.all_to_all(send, "expert", split_axis=0, concat_axis=0, tiled=True)
    flat_rows = received.reshape(-1, model_dim)
    hidden_units = jax.nn.gelu(
        jnp.dot(flat_rows, up_weight[0], preferred_element_type=jnp.float32), approximate=True
    ).astype(jnp.bfloat16)
    expert_out = jnp.dot(hidden_units, down_weight[0], preferred_element_type=jnp.float32).astype(
        jnp.bfloat16
    )
    projected = jnp.dot(expert_out, out_weight, preferred_element_type=jnp.float32)
    projected = projected.reshape(num_experts, capacity, lat_dim)
    returned = lax.all_to_all(projected, "expert", split_axis=0, concat_axis=0, tiled=True)
    gated = lax.dot_general(
        weighted,
        returned.reshape(-1, lat_dim),
        (((0,), (0,)), ((), ())),
        precision=lax.Precision.HIGHEST,
        preferred_element_type=jnp.float32,
    )
    latent = jnp.dot(frames, out_weight, preferred_element_type=jnp.float32) + gated
    latent_low = latent.astype(jnp.bfloat16)

    padded = edge_rows(latent_low, 4)
    num_seg = lax.axis_size("seg")
    spread = jnp.broadcast_to(padded[None], (num_seg,) + padded.shape)
    sequences = lax.all_to_all(spread, "seg", split_axis=0, concat_axis=0, tiled=True)
    first_in = conv_seven(sequences, in_conv, tok_rows + 2)
    act_first = snake_act(first_in, snake_first * PI_INV, 1.0 / snake_first)
    slab = lax.axis_index("expert")
    frame = slab * tok_rows - 1 + jnp.arange(tok_rows + 2, dtype=jnp.int32)
    inside = (frame >= 0) & (frame < num_experts * tok_rows)
    act_first = jnp.where(inside[None, :, None], act_first, 0.0).astype(jnp.bfloat16)
    return upsample(act_first, first_up, tok_rows)


def solution(mesh):
    placed = (
        P(("seg", "expert"), None),
        P(("seg", "expert"), None),
        P(("seg", "expert"), None),
        P("expert", None, None),
        P("expert", None, None),
        P(),
        P(),
        P(),
        P(None, None, "seg"),
    )
    return jax.shard_map(
        local, mesh=mesh, in_specs=placed, out_specs=P(None, "expert", "seg"), check_vma=False
    )
```

time: 226 us -> 136 us (0.60)
  waiting for transfers between devices: 89.4 us -> 47.4 us
  blocking collectives: 41 us -> 0 us
  between operations: 13.7 us -> 0.22 us
  starting transfers between devices: 13.6 us -> 22.3 us
  local copies, waits for them, and re-layouts: 21.4 us -> 15.9 us
  matrix products: 42.3 us -> 46.6 us
  other arithmetic: 3.95 us -> 1.44 us
    all_gather x1 -> x0, waiting for transfers between devices: 52.8 us -> none  [local(): lax.all_gather(pad_first[None], 'seg', axis=0, tiled=True)]
    all_to_all x1 -> x0, blocking collectives: 41 us -> none  [local(): lax.all_to_all(send_buffer, 'expert', split_axis=0, concat_axis=0, tiled=...]
    all_to_all x1 -> x3, waiting for transfers between devices: 31.1 us -> 44.4 us  [the longest x1 30.8 us: local(): lax.all_to_all(send, 'expert', split_axis=0, concat_axis=0, tiled=True)]
    all_to_all x1 -> x3, starting transfers between devices: 4.72 us -> 18 us  [the longest x1 9.47 us: local(): lax.all_to_all(send, 'expert', split_axis=0, concat_axis=0, tiled=True)]
    gather x1 -> x0, local copies, waits for them, and re-layouts: 5.57 us -> none  [local(): picked_rows = returned.reshape(num_experts * capacity, model_dim)[dest_slot]]
    scatter x1 -> x0, local copies, waits for them, and re-layouts: 5.52 us -> none  [local(): jnp.zeros((num_experts * capacity, model_dim), jnp.bfloat16).at[dest_slot]]
    dot_general x2 -> x5, matrix products: 18.1 us -> 23.4 us  [the longest x1 16.7 us: local(): jnp.dot(hidden_units, down_weight[0], preferred_element_type=jnp.float32)]
    ppermute x4 -> x2, starting transfers between devices: 8.86 us -> 4.31 us  [the longest x1 2.29 us: edge_rows(): before = lax.ppermute(value[-width:], 'expert', up)]
  transfers between devices with their start and end apart: 6 -> 5, of which waited for: 4 -> 4; matrix products, arithmetic and copies ran while one was open for 0% -> 0% of each run, Pallas kernels for 0% -> 0%
where the time goes in v1:
time: 136 us; the launch traced here: 134 us
  waiting for transfers between devices  47.4 us (35%)
  matrix products  46.6 us (34%)
  starting transfers between devices  22.3 us (16%)
  local copies, waits for them, and re-layouts  15.9 us (12%)
  other arithmetic  1.44 us (1%)
    all_to_all x1, waiting for transfers between devices, local(): lax.all_to_all(send, 'expert', split_axis=0, concat_axis=0, tiled=True)  30.8 us
    dot_general x1, matrix products, local(): jnp.dot(hidden_units, down_weight[0], preferred_element_type=jnp.float32)  16.7 us
    all_to_all x1, starting transfers between devices, local(): lax.all_to_all(send, 'expert', split_axis=0, concat_axis=0, tiled=True)  9.47 us
    all_to_all x1, waiting for transfers between devices, local(): lax.all_to_all(projected, 'expert', split_axis=0, concat_axis=0, tiled=True)  8.4 us
    dot_general x1, matrix products, conv_seven(): jnp.einsum('klc,co->klo', stacked, weights.reshape(-1, weights.shape[2]),...  8.19 us
    dot_general x1, matrix products, upsample(): jnp.einsum('klc,rco->klro', here_rows, weights[4:12], preferred_element_t...  6.77 us
    all_to_all x1, waiting for transfers between devices, local(): lax.all_to_all(spread, 'seg', split_axis=0, concat_axis=0, tiled=True)  5.17 us
    unnamed x19, local copies, waits for them, and re-layouts  5.11 us
  transfers between devices with their start and end apart: 5, of which 4 were waited for; matrix products, arithmetic and copies ran while one was open for 0% of the time, Pallas kernels for 0%

profile of v1, /device:TPU:1, one launch (start us, length us, event | category | flops | bytes accessed | tf_op | source)
XLA Modules:
  0.0 133.8 jit_solution(10981148172381297585)
XLA Ops:
  0.0 0.9 fusion.61
  1.4 3.3 %convolution_convert_fusion = bf16[768,1536]{1,0:T(8,128)(2,1)} fusion(pred[768,256]{1,0:T(32,128)(4,1)S(1)} %fusion.39, bf16[256,1536]{1,0:T(8,128)(2,1)} %param.9), kind=kOutput, calls=%fused_computation.27 | convolution fusion | flops 605159424 | bytes 3342336 | tf_op jit(solution)/shard_map/dot_general | solution.py:94
  4.7 9.5 %all-to-all-start = ((bf16[32,24,1536]{2,1,0:T(8,128)(2,1)}), bf16[32,24,1536]{2,1,0:T(8,128)(2,1)}, u32[]{:S(2)}, u32[]{:S(2)}) async-start(bf16[32,24,1536]{2,1,0:T(8,128)(2,1)} %bitcast.76), calls=%async_computation | async-start | bytes 4718592 | tf_op jit(solution)/shard_map/all_to_all | solution.py:98
  14.2 0.4 fusion.62
  14.6 30.8 %all-to-all-done = bf16[32,24,1536]{2,1,0:T(8,128)(2,1)} async-done(((bf16[32,24,1536]{2,1,0:T(8,128)(2,1)}), bf16[32,24,1536]{2,1,0:T(8,128)(2,1)}, u32[]{:S(2)}, u32[]{:S(2)}) %all-to-all-start) | async-done | bytes 2359328 | tf_op jit(solution)/shard_map/all_to_all | solution.py:98
  45.4 16.7 %fusion.18 = bf16[768,1536]{1,0:T(8,128)(2,1)} fusion(bf16[1,2048,1536]{2,1,0:T(8,128)(2,1)} %param.13, bf16[768,1536]{1,0:T(8,128)(2,1)} %bitcast.7, bf16[1,1536,2048]{2,1,0:T(8,128)(2,1)} %param.12), kind=kOutput, calls=%fused_computation.26 | convolution fusion | flops 9679011840 | bytes 17301504 | tf_op jit(solution)/shard_map/dot_general | solution.py:103
  62.0 2.4 %fusion.63 = f32[768,64]{1,0:T(8,128)S(1)} fusion(bf16[768,1536]{1,0:T(8,128)(2,1)} %fusion.18, bf16[1536,64]{0,1:T(8,128)(2,1)S(1)} %copy-done.2), kind=kOutput, calls=%fused_computation.73 | convolution fusion | flops 150994944 | bytes 2752512 | tf_op jit(solution)/shard_map/dot_general | solution.py:106
  64.5 0.9 reshape.155
  65.4 4.3 %all-to-all-start.1 = ((f32[32,1,1536]{2,1,0:T(1,128)}), f32[32,1,1536]{2,1,0:T(1,128)S(1)}, u32[]{:S(2)}, u32[]{:S(2)}) async-start(f32[32,1,1536]{2,1,0:T(1,128)} %reshape.155), calls=%async_computation.1 | async-start | bytes 393216 | tf_op jit(solution)/shard_map/all_to_all | solution.py:108
  69.8 8.4 %all-to-all-done.1 = f32[32,1,1536]{2,1,0:T(1,128)S(1)} async-done(((f32[32,1,1536]{2,1,0:T(1,128)}), f32[32,1,1536]{2,1,0:T(1,128)S(1)}, u32[]{:S(2)}, u32[]{:S(2)}) %all-to-all-start.1) | async-done | bytes 196640 | tf_op jit(solution)/shard_map/all_to_all | solution.py:108
  78.2 0.5 broadcast.70
  78.7 1.1 reduce
  79.9 0.9 fusion.37
  80.9 2.3 %collective-permute-start = (bf16[4,64]{0,1:T(8,128)(2,1)S(1)}, bf16[4,64]{0,1:T(8,128)(2,1)S(1)}, u32[]{:S(2)}, u32[]{:S(2)}) collective-permute-start(bf16[4,64]{0,1:T(8,128)(2,1)S(1)} %get-tuple-element.12), channel_id=1, source_target_pairs={{0,1},{1,2},{2,3},{3,4},{4,5},{5,6},{6,7},{7,8},{8,9},{9,10},{10,1... | collective-permute-start | bytes 1544 | tf_op jit(solution)/shard_map/ppermute | solution.py:31
  83.2 2.0 %collective-permute-start.1 = (bf16[4,64]{0,1:T(8,128)(2,1)S(1)}, bf16[4,64]{0,1:T(8,128)(2,1)S(1)}, u32[]{:S(2)}, u32[]{:S(2)}) collective-permute-start(bf16[4,64]{0,1:T(8,128)(2,1)S(1)} %get-tuple-element.13), channel_id=1, source_target_pairs={{1,0},{2,1},{3,2},{4,3},{5,4},{6,5},{7,6},{8,7},{9,8},{10,9},{11,1... | collective-permute-start | bytes 1544 | tf_op jit(solution)/shard_map/ppermute | solution.py:32
  85.2 3.0 %collective-permute-done.1 = bf16[4,64]{0,1:T(8,128)(2,1)S(1)} collective-permute-done((bf16[4,64]{0,1:T(8,128)(2,1)S(1)}, bf16[4,64]{0,1:T(8,128)(2,1)S(1)}, u32[]{:S(2)}, u32[]{:S(2)}) %collective-permute-start.1) | collective-permute-done | bytes 544 | tf_op jit(solution)/shard_map/ppermute | solution.py:32
  88.3 0.7 broadcast_in_dim.70
  89.0 4.2 %all-to-all-start.2 = ((bf16[4,264,64]{1,2,0:T(8,128)(2,1)}), bf16[4,264,64]{1,2,0:T(8,128)(2,1)S(1)}, u32[]{:S(2)}, u32[]{:S(2)}) async-start(bf16[4,264,64]{1,2,0:T(8,128)(2,1)} %broadcast_in_dim.70), calls=%async_computation.2 | async-start | bytes 393216 | tf_op jit(solution)/shard_map/all_to_all | solution.py:122
  93.2 5.2 %all-to-all-done.2 = bf16[4,264,64]{1,2,0:T(8,128)(2,1)S(1)} async-done(((bf16[4,264,64]{1,2,0:T(8,128)(2,1)}), bf16[4,264,64]{1,2,0:T(8,128)(2,1)S(1)}, u32[]{:S(2)}, u32[]{:S(2)}) %all-to-all-start.2) | async-done | bytes 135200 | tf_op jit(solution)/shard_map/all_to_all | solution.py:122
  98.4 1.1 fusion.58
  99.7 0.2 copy.35
  99.9 0.2 copy.34
  100.1 0.2 copy.33
  100.4 0.2 copy.32
  100.6 1.1 copy.31
  101.7 1.8 %copy.30 = bf16[4,258,64]{2,1,0:T(8,128)(2,1)} copy(bf16[4,258,64]{1,2,0:T(8,128)(2,1)} %get-tuple-element.11) | data formatting | bytes 264192
  103.5 3.0 %concatenate.10 = bf16[4,258,448]{2,1,0:T(8,128)(2,1)} concatenate(bf16[4,258,64]{2,1,0:T(8,128)(2,1)} %copy.30, bf16[4,258,64]{2,1,0:T(8,128)(2,1)S(1)} %copy.31, bf16[4,258,64]{2,1,0:T(8,128)(2,1)S(1)} %copy.32, bf16[4,258,64]{2,1,0:T(8,128)(2,1)S(1)} %copy.33, bf16[4,258,64]{2,1,0:T(8,128)(2,1)S(1)} %copy.34, bf16[4,258,64]{2,1,0:T(8,128)(2,1)S(1)} %copy.35, ...), dimensions={2} | concatenate | bytes 1849344 | tf_op jit(solution)/shard_map/concatenate | solution.py:38
  106.5 8.2 %select_convert_fusion = bf16[4,258,2048]{2,1,0:T(8,128)(2,1)S(1)} fusion(f32[2048]{0:T(1024)S(1)} %get-tuple-element.15, f32[2048]{0:T(1024)S(1)} %get-tuple-element.14, pred[258]{0:T(512)(128)(4,1)S(1)} %fusion.51, bf16[4,258,448]{2,1,0:T(8,128)(2,1)} %concatenate.10, bf16[448,2048,1]{1,0,2:T(8,128)(2,1)S(1)} %bitcast.75), kind=kOutput, calls=%fused_computation.3 | convolution fusion | flops 1935998976 | bytes 7003394 | tf_op jit(solution)/shard_map/klc,co->klo/dot_general | solution.py:39
  114.7 3.9 %fusion.13 = f32[4,256,4,128]{3,1,2,0:T(8,128)S(1)} fusion(bf16[4,258,2048]{2,1,0:T(8,128)(2,1)S(1)} %select_convert_fusion, bf16[16,2048,128]{2,1,0:T(8,128)(2,1)} %param.17), kind=kOutput, calls=%fused_computation.17 | convolution fusion | flops 2147483648 | bytes 8388608 | tf_op jit(solution)/shard_map/klc,rco->klro/dot_general | solution.py:57
  118.7 3.9 %fusion.14 = f32[4,256,4,128]{3,1,2,0:T(8,128)S(1)} fusion(bf16[4,258,2048]{2,1,0:T(8,128)(2,1)S(1)} %select_convert_fusion, bf16[16,2048,128]{2,1,0:T(8,128)(2,1)} %param.17), kind=kOutput, calls=%fused_computation.19 | convolution fusion | flops 2147483648 | bytes 8388608 | tf_op jit(solution)/shard_map/klc,rco->klro/dot_general | solution.py:54
  122.6 6.8 %maximum_add_fusion = f32[4,256,8,128]{3,1,2,0:T(8,128)S(1)} fusion(f32[4,256,4,128]{3,1,2,0:T(8,128)S(1)} %fusion.13, f32[4,256,4,128]{3,1,2,0:T(8,128)S(1)} %fusion.14, bf16[16,2048,128]{2,1,0:T(8,128)(2,1)} %param.17, bf16[4,258,2048]{2,1,0:T(8,128)(2,1)S(1)} %select_convert_fusion), kind=kOutput, calls=%fused_computation.22 | convolution fusion | flops 4297064448 | bytes 16777216 | tf_op jit(solution)/shard_map/klc,rco->klro/dot_general | solution.py:51
  129.4 4.4 %copy.38 = f32[4,256,8,128]{3,2,1,0:T(8,128)} copy(f32[4,256,8,128]{3,1,2,0:T(8,128)S(1)} %maximum_add_fusion) | data formatting | bytes 8388608 | tf_op jit(solution)/shard_map/add | solution.py:60
  (25 shorter events, 1.0 us)
Async XLA Ops:
  0.0 106.5 %copy-start = (bf16[7,64,2048]{2,1,0:T(8,128)(2,1)S(1)}, bf16[7,64,2048]{2,1,0:T(8,128)(2,1)}, u32[]{:S(2)}) copy-start(bf16[7,64,2048]{2,1,0:T(8,128)(2,1)} %param.15) | copy-start | bytes 5505028
  0.0 14.2 %copy-start.1 = (bf16[256,1536]{1,0:T(8,128)(2,1)S(1)}, bf16[256,1536]{1,0:T(8,128)(2,1)}, u32[]{:S(2)}) copy-start(bf16[256,1536]{1,0:T(8,128)(2,1)} %param.9) | copy-start | bytes 2359300
  0.0 14.2 %copy-start.4 = (f32[256,2]{0,1:T(2,128)S(1)}, f32[256,2]{0,1:T(2,128)}, u32[]{:S(2)}) copy-start(f32[256,2]{0,1:T(2,128)} %param.11) | copy-start | bytes 6148
  0.0 14.2 %copy-start.2 = (bf16[1536,64]{0,1:T(8,128)(2,1)S(1)}, bf16[1536,64]{0,1:T(8,128)(2,1)}, u32[]{:S(2)}) copy-start(bf16[1536,64]{0,1:T(8,128)(2,1)} %param.14) | copy-start | bytes 589828
  4.7 40.7 %all-to-all-start = ((bf16[32,24,1536]{2,1,0:T(8,128)(2,1)}), bf16[32,24,1536]{2,1,0:T(8,128)(2,1)}, u32[]{:S(2)}, u32[]{:S(2)}) async-start(bf16[32,24,1536]{2,1,0:T(8,128)(2,1)} %bitcast.76), calls=%async_computation | async-start | bytes 4718592 | tf_op jit(solution)/shard_map/all_to_all | solution.py:98
  45.4 39.8 %copy-start.3 = (f32[2048]{0:T(1024)S(1)}, f32[2048]{0:T(1024)}, u32[]{:S(2)}) copy-start(f32[2048]{0:T(1024)} %param.16) | copy-start | bytes 24580
  65.4 12.8 %all-to-all-start.1 = ((f32[32,1,1536]{2,1,0:T(1,128)}), f32[32,1,1536]{2,1,0:T(1,128)S(1)}, u32[]{:S(2)}, u32[]{:S(2)}) async-start(f32[32,1,1536]{2,1,0:T(1,128)} %reshape.155), calls=%async_computation.1 | async-start | bytes 393216 | tf_op jit(solution)/shard_map/all_to_all | solution.py:108
  80.9 4.4 %collective-permute-start = (bf16[4,64]{0,1:T(8,128)(2,1)S(1)}, bf16[4,64]{0,1:T(8,128)(2,1)S(1)}, u32[]{:S(2)}, u32[]{:S(2)}) collective-permute-start(bf16[4,64]{0,1:T(8,128)(2,1)S(1)} %get-tuple-element.12), channel_id=1, source_target_pairs={{0,1},{1,2},{2,3},{3,4},{4,5},{5,6},{6,7},{7,8},{8,9},{9,10},{10,1... | collective-permute-start | bytes 1544 | tf_op jit(solution)/shard_map/ppermute | solution.py:31
  83.2 5.1 %collective-permute-start.1 = (bf16[4,64]{0,1:T(8,128)(2,1)S(1)}, bf16[4,64]{0,1:T(8,128)(2,1)S(1)}, u32[]{:S(2)}, u32[]{:S(2)}) collective-permute-start(bf16[4,64]{0,1:T(8,128)(2,1)S(1)} %get-tuple-element.13), channel_id=1, source_target_pairs={{1,0},{2,1},{3,2},{4,3},{5,4},{6,5},{7,6},{8,7},{9,8},{10,9},{11,1... | collective-permute-start | bytes 1544 | tf_op jit(solution)/shard_map/ppermute | solution.py:32
  89.0 9.4 %all-to-all-start.2 = ((bf16[4,264,64]{1,2,0:T(8,128)(2,1)}), bf16[4,264,64]{1,2,0:T(8,128)(2,1)S(1)}, u32[]{:S(2)}, u32[]{:S(2)}) async-start(bf16[4,264,64]{1,2,0:T(8,128)(2,1)} %broadcast_in_dim.70), calls=%async_computation.2 | async-start | bytes 393216 | tf_op jit(solution)/shard_map/all_to_all | solution.py:122

commit v2 on v1

--- a/solution.py
+++ b/solution.py
@@ -1,6 +1,8 @@
 import jax
 import jax.numpy as jnp
 from jax import lax
+from jax.experimental import pallas as pl
+from jax.experimental.pallas import tpu as pltpu
 from jax.sharding import PartitionSpec as P
 
 SIN2 = (
@@ -12,9 +14,10 @@
     -3.3565926551818848,
 )
 PI_INV = 0.3183098861837907
-
-
-def snake_act(values, freq, inv_alpha):
+SEQS = 4
+
+
+def snake(values, freq, inv_alpha):
     turns = values * freq
     frac = turns - jnp.round(turns)
     t = frac * frac
@@ -33,32 +36,123 @@
     return jnp.concatenate([before, value, after], axis=0)
 
 
-def conv_seven(padded, weights, length):
-    windows = [lax.slice_in_dim(padded, tap, tap + length, axis=1) for tap in range(7)]
-    stacked = jnp.concatenate(windows, axis=2)
-    return jnp.einsum(
-        "klc,co->klo",
-        stacked,
-        weights.reshape(-1, weights.shape[2]),
-        preferred_element_type=jnp.float32,
-    )
-
-
-def upsample(padded, weights, length):
-    prev_rows = padded[:, 0:length]
-    here_rows = padded[:, 1 : length + 1]
-    next_rows = padded[:, 2 : length + 2]
-    middle = jnp.einsum(
-        "klc,rco->klro", here_rows, weights[4:12], preferred_element_type=jnp.float32
-    )
-    early_part = jnp.einsum(
-        "klc,rco->klro", prev_rows, weights[12:16], preferred_element_type=jnp.float32
-    )
-    later_part = jnp.einsum(
-        "klc,rco->klro", next_rows, weights[0:4], preferred_element_type=jnp.float32
-    )
-    joined = middle + jnp.concatenate([early_part, later_part], axis=2)
-    return joined.reshape(padded.shape[0], length * 8, weights.shape[2])
+def decode_kernel(
+    main_ref, edge_ref, freq_ref, inv_ref, conv_hbm, up_hbm, out_hbm,
+    plain, pairs, cols, rims, wide, act, here, other, tile, conv_w, up_w, in_sems, out_sems,
+):
+    rows = main_ref.shape[1] * 2
+    total = SEQS * rows
+    get_conv = pltpu.make_async_copy(conv_hbm, conv_w.at[pl.ds(0, 448)], in_sems.at[0])
+    get_conv.start()
+    get_up = pltpu.make_async_copy(up_hbm, up_w, in_sems.at[1])
+    get_up.start()
+    slab = lax.axis_index("expert")
+    keep_left = jnp.where(slab == 0, 0.0, 1.0)
+    keep_right = jnp.where(slab == lax.axis_size("expert") - 1, 0.0, 1.0)
+    conv_w[pl.ds(448, 64), :] = jnp.zeros((64, conv_w.shape[1]), jnp.bfloat16)
+    plain[...] = jnp.zeros_like(plain)
+    rims[...] = jnp.zeros_like(rims)
+    for s in range(SEQS):
+        body = main_ref[s].astype(jnp.float32)
+        half = rows // 2
+        plain[pl.ds(8, half), 0:64] = body[:, 0:64]
+        plain[pl.ds(8 + half, half), 0:64] = body[:, 64:128]
+        plain[pl.ds(0, 8), 0:64] = edge_ref[s, 0][:, 0:64] * keep_left
+        plain[pl.ds(8 + rows, 8), 0:64] = edge_ref[s, 1][:, 0:64] * keep_right
+        pairs[...] = plain[pl.ds(0, rows + 16), :] + pltpu.roll(
+            plain[pl.ds(1, rows + 16), :], 64, axis=1
+        )
+        for m in range(4):
+            lanes = slice(128 * m, 128 * m + 128)
+            cols[pl.ds(s * rows, rows), lanes] = pairs[pl.ds(5 + 2 * m, rows), :].astype(jnp.bfloat16)
+            rims[pl.ds(2 * s, 1), lanes] = pairs[pl.ds(4 + 2 * m, 1), :]
+            rims[pl.ds(2 * s + 1, 1), lanes] = pairs[pl.ds(5 + 2 * m + rows, 1), :]
+    cols[pl.ds(total, 16), :] = rims[...].astype(jnp.bfloat16)
+    get_conv.wait()
+
+    @pl.loop(0, act.shape[1] // 256)
+    def _(n):
+        lanes = pl.ds(pl.multiple_of(n * 256, 256), 256)
+        freq = freq_ref[:, lanes]
+        inv = inv_ref[:, lanes]
+        weight = conv_w[:, lanes]
+        for part, size in [(s * rows, rows) for s in range(SEQS)] + [(total, 16)]:
+            value = jnp.dot(
+                cols[pl.ds(part, size), :], weight, preferred_element_type=jnp.float32
+            )
+            act[pl.ds(part, size), lanes] = snake(value, freq, inv).astype(jnp.bfloat16)
+
+    line = lax.broadcasted_iota(jnp.int32, (16, 1), 0)
+    gone = jnp.where(line % 2 == 0, keep_left, keep_right)
+    edge_act = act[pl.ds(total, 16), :].astype(jnp.float32) * gone
+    act[pl.ds(total, 16), :] = edge_act.astype(jnp.bfloat16)
+    get_up.wait()
+
+    for q in range(4):
+        r = 2 * q
+        tap = (r + 12) % 16
+        near = jnp.concatenate([up_w[r + 4], up_w[r + 5]], axis=1)
+        far = jnp.concatenate([up_w[tap], up_w[tap + 1]], axis=1)
+        rim = jnp.dot(act[pl.ds(total, 16), :], far, preferred_element_type=jnp.float32)
+        for s in range(SEQS):
+            block = act[pl.ds(s * rows, rows), :]
+            here[...] = jnp.dot(block, near, preferred_element_type=jnp.float32)
+            other[pl.ds(8, rows), :] = jnp.dot(block, far, preferred_element_type=jnp.float32)
+            if q < 2:
+                other[pl.ds(7, 1), :] = rim[2 * s : 2 * s + 1]
+                shifted = other[pl.ds(7, rows), :]
+            else:
+                other[pl.ds(8 + rows, 1), :] = rim[2 * s + 1 : 2 * s + 2]
+                shifted = other[pl.ds(9, rows), :]
+            both = here[...] + shifted
+            tile[s, pl.ds(r, rows, stride=8), :] = both[:, 0:128]
+            tile[s, pl.ds(r + 1, rows, stride=8), :] = both[:, 128:256]
+    puts = [
+        pltpu.make_async_copy(tile.at[s], out_hbm.at[s], out_sems.at[s]) for s in range(SEQS)
+    ]
+    for put in puts:
+        put.start()
+    for put in puts:
+        put.wait()
+
+
+def decode(main, edges, in_conv, snake_first, first_up):
+    channels = in_conv.shape[2]
+    rows = main.shape[1] * 2
+    total = SEQS * rows + 16
+    vmem = pl.BlockSpec(memory_space=pltpu.VMEM)
+    anywhere = pl.BlockSpec(memory_space=pl.ANY)
+    return pl.pallas_call(
+        decode_kernel,
+        out_shape=jax.ShapeDtypeStruct((SEQS, rows * 8, first_up.shape[2]), jnp.float32),
+        in_specs=[vmem, vmem, vmem, vmem, anywhere, anywhere],
+        out_specs=anywhere,
+        scratch_shapes=[
+            pltpu.VMEM((rows + 24, 128), jnp.float32),
+            pltpu.VMEM((rows + 16, 128), jnp.float32),
+            pltpu.VMEM((total, 512), jnp.bfloat16),
+            pltpu.VMEM((16, 512), jnp.float32),
+            pltpu.VMEM((8, 128), jnp.float32),
+            pltpu.VMEM((total, channels), jnp.bfloat16),
+            pltpu.VMEM((rows, 256), jnp.float32),
+            pltpu.VMEM((rows + 16, 256), jnp.float32),
+            pltpu.VMEM((SEQS, rows * 8, first_up.shape[2]), jnp.float32),
+            pltpu.VMEM((512, channels), jnp.bfloat16),
+            pltpu.VMEM(first_up.shape, jnp.bfloat16),
+            pltpu.SemaphoreType.DMA((2,)),
+            pltpu.SemaphoreType.DMA((SEQS,)),
+        ],
+        compiler_params=pltpu.CompilerParams(vmem_limit_bytes=48 << 20),
+        cost_estimate=pl.CostEstimate(flops=11 * 10**9, bytes_accessed=16 << 20, transcendentals=0),
+        name="decode",
+    )(
+        main,
+        edges,
+        (snake_first * PI_INV)[None, :],
+        (1.0 / snake_first)[None, :],
+        in_conv.reshape(-1, channels),
+        first_up,
+    )
 
 
 def local(
@@ -120,13 +214,12 @@
     num_seg = lax.axis_size("seg")
     spread = jnp.broadcast_to(padded[None], (num_seg,) + padded.shape)
     sequences = lax.all_to_all(spread, "seg", split_axis=0, concat_axis=0, tiled=True)
-    first_in = conv_seven(sequences, in_conv, tok_rows + 2)
-    act_first = snake_act(first_in, snake_first * PI_INV, 1.0 / snake_first)
-    slab = lax.axis_index("expert")
-    frame = slab * tok_rows - 1 + jnp.arange(tok_rows + 2, dtype=jnp.int32)
-    inside = (frame >= 0) & (frame < num_experts * tok_rows)
-    act_first = jnp.where(inside[None, :, None], act_first, 0.0).astype(jnp.bfloat16)
-    return upsample(act_first, first_up, tok_rows)
+    half = tok_rows // 2
+    main = jnp.concatenate([sequences[:, 4 : 4 + half], sequences[:, 4 + half : 4 + tok_rows]], axis=2)
+    left = jnp.pad(sequences[:, 0:4], ((0, 0), (4, 0), (0, 64)))
+    right = jnp.pad(sequences[:, 4 + tok_rows :], ((0, 0), (0, 4), (0, 64)))
+    edges = jnp.stack([left, right], axis=1).astype(jnp.float32)
+    return decode(main, edges, in_conv, snake_first, first_up)
 
 
 def solution(mesh):

time: 136 us -> 120 us (0.88)
  matrix products: 46.6 us -> 22.8 us
  Pallas kernels: 0 us -> 19.4 us
  local copies, waits for them, and re-layouts: 15.9 us -> 4.58 us
  other arithmetic: 1.44 us -> 2.83 us
    dot_general x4 -> x0, matrix products: 22.8 us -> none  [the longest x1 8.19 us: conv_seven(): jnp.einsum('klc,co->klo', stacked, weights.reshape(-1, weights.shape[2]),...]
    pallas_call x0 -> x1, Pallas kernels: none -> 19.4 us  [decode(): pl.pallas_call(decode_kernel, out_shape=jax.ShapeDtypeStruct((SEQS, rows...]
    add x1 -> x0, local copies, waits for them, and re-layouts: 4.44 us -> none  [upsample(): joined = middle + jnp.concatenate([early_part, later_part], axis=2)]
    unnamed x19 -> x16, local copies, waits for them, and re-layouts: 5.11 us -> 1.54 us
    concatenate x1 -> x0, local copies, waits for them, and re-layouts: 2.99 us -> none  [conv_seven(): stacked = jnp.concatenate(windows, axis=2)]
  transfers between devices with their start and end apart: 5 -> 5, of which waited for: 4 -> 4; matrix products, arithmetic and copies ran while one was open for 0% -> 1% of each run, Pallas kernels for 0% -> 0%
where the time goes in v2:
time: 120 us; the launch traced here: 119 us
  waiting for transfers between devices  46.7 us (39%)
  matrix products  22.8 us (19%)
  starting transfers between devices  22.3 us (19%)
  Pallas kernels  19.4 us (16%)
  local copies, waits for them, and re-layouts  4.58 us (4%)
  other arithmetic  2.83 us (2%)
    all_to_all x1, waiting for transfers between devices, local(): lax.all_to_all(send, 'expert', split_axis=0, concat_axis=0, tiled=True)  30.8 us
    pallas_call x1, Pallas kernels, decode(): pl.pallas_call(decode_kernel, out_shape=jax.ShapeDtypeStruct((SEQS, rows...  19.4 us
    dot_general x1, matrix products, local(): jnp.dot(hidden_units, down_weight[0], preferred_element_type=jnp.float32)  16 us
    all_to_all x1, starting transfers between devices, local(): lax.all_to_all(send, 'expert', split_axis=0, concat_axis=0, tiled=True)  9.42 us
    all_to_all x1, waiting for transfers between devices, local(): lax.all_to_all(projected, 'expert', split_axis=0, concat_axis=0, tiled=True)  8.4 us
    all_to_all x1, waiting for transfers between devices, local(): lax.all_to_all(spread, 'seg', split_axis=0, concat_axis=0, tiled=True)  4.48 us
    all_to_all x1, starting transfers between devices, local(): lax.all_to_all(projected, 'expert', split_axis=0, concat_axis=0, tiled=True)  4.35 us
    all_to_all x1, starting transfers between devices, local(): lax.all_to_all(spread, 'seg', split_axis=0, concat_axis=0, tiled=True)  4.19 us
  transfers between devices with their start and end apart: 5, of which 4 were waited for; matrix products, arithmetic and copies ran while one was open for 1% of the time, Pallas kernels for 0%

profile of v2, /device:TPU:1, one launch (start us, length us, event | category | flops | bytes accessed | tf_op | source)
XLA Modules:
  0.0 118.9 jit_solution(16219940604833890704)
XLA Ops:
  0.0 0.8 fusion.47
  0.8 0.1 fusion.35
  1.0 0.6 iota_convert_fusion
  1.6 0.7 eq.80
  2.3 0.2 fusion.27
  2.6 2.2 %convolution_convert_fusion = bf16[768,1536]{1,0:T(8,128)(2,1)} fusion(pred[768,256]{1,0:T(32,128)(4,1)S(1)} %fusion.27, bf16[256,1536]{1,0:T(8,128)(2,1)S(1)} %copy-done), kind=kOutput, calls=%fused_computation.14 | convolution fusion | flops 605159424 | bytes 3342336 | tf_op jit(solution)/shard_map/dot_general | solution.py:188
  4.7 9.4 %all-to-all-start = ((bf16[32,24,1536]{2,1,0:T(8,128)(2,1)}), bf16[32,24,1536]{2,1,0:T(8,128)(2,1)S(1)}, u32[]{:S(2)}, u32[]{:S(2)}) async-start(bf16[32,24,1536]{2,1,0:T(8,128)(2,1)} %bitcast.6), calls=%async_computation | async-start | bytes 4718592 | tf_op jit(solution)/shard_map/all_to_all | solution.py:192
  14.2 0.4 fusion.48
  14.6 30.8 %all-to-all-done = bf16[32,24,1536]{2,1,0:T(8,128)(2,1)S(1)} async-done(((bf16[32,24,1536]{2,1,0:T(8,128)(2,1)}), bf16[32,24,1536]{2,1,0:T(8,128)(2,1)S(1)}, u32[]{:S(2)}, u32[]{:S(2)}) %all-to-all-start) | async-done | bytes 2359328 | tf_op jit(solution)/shard_map/all_to_all | solution.py:192
  45.3 16.0 %fusion.12 = bf16[768,1536]{1,0:T(8,128)(2,1)} fusion(bf16[1,2048,1536]{2,1,0:T(8,128)(2,1)} %param.13, bf16[768,1536]{1,0:T(8,128)(2,1)S(1)} %bitcast.49, bf16[1,1536,2048]{2,1,0:T(8,128)(2,1)} %param.12), kind=kOutput, calls=%fused_computation.13 | convolution fusion | flops 9679011840 | bytes 17301504 | tf_op jit(solution)/shard_map/dot_general | solution.py:197
  61.3 2.5 %fusion.49 = f32[768,64]{1,0:T(8,128)S(1)} fusion(bf16[768,1536]{1,0:T(8,128)(2,1)} %fusion.12, bf16[1536,64]{0,1:T(8,128)(2,1)S(1)} %copy-done.2), kind=kOutput, calls=%fused_computation.57 | convolution fusion | flops 150994944 | bytes 2752512 | tf_op jit(solution)/shard_map/dot_general | solution.py:200
  63.9 0.9 reshape.135
  64.8 4.4 %all-to-all-start.1 = ((f32[32,1,1536]{2,1,0:T(1,128)}), f32[32,1,1536]{2,1,0:T(1,128)S(1)}, u32[]{:S(2)}, u32[]{:S(2)}) async-start(f32[32,1,1536]{2,1,0:T(1,128)} %reshape.135), calls=%async_computation.1 | async-start | bytes 393216 | tf_op jit(solution)/shard_map/all_to_all | solution.py:202
  69.1 8.4 %all-to-all-done.1 = f32[32,1,1536]{2,1,0:T(1,128)S(1)} async-done(((f32[32,1,1536]{2,1,0:T(1,128)}), f32[32,1,1536]{2,1,0:T(1,128)S(1)}, u32[]{:S(2)}, u32[]{:S(2)}) %all-to-all-start.1) | async-done | bytes 196640 | tf_op jit(solution)/shard_map/all_to_all | solution.py:202
  77.5 0.5 broadcast.60
  78.1 1.1 reduce
  79.2 0.1 reshape.136
  79.3 1.6 %fusion.25 = bf16[256,64]{0,1:T(8,128)(2,1)S(1)} fusion(f32[256,64]{0,1:T(8,128)S(1)} %fusion.48, f32[32,24,64]{2,1,0:T(8,128)S(1)} %reshape.136, f32[32,256]{1,0:T(8,128)S(1)} %select_add_fusion, f32[32,256]{1,0:T(8,128)S(1)} %fusion.35, f32[24]{0:T(128)} %iota_convert_fusion, pred[32,256]{1,0:T(8,128)(4,1)} %copy-done.3), kind=kOutput, calls=%fused_computation.21 | convolution fusion | flops 151617536 | bytes 368736 | tf_op jit(solution)/shard_map/dot_general | solution.py:203
  81.0 2.3 %collective-permute-start = (bf16[4,64]{0,1:T(8,128)(2,1)S(1)}, bf16[4,64]{0,1:T(8,128)(2,1)S(1)}, u32[]{:S(2)}, u32[]{:S(2)}) collective-permute-start(bf16[4,64]{0,1:T(8,128)(2,1)S(1)} %get-tuple-element.9), channel_id=1, source_target_pairs={{0,1},{1,2},{2,3},{3,4},{4,5},{5,6},{6,7},{7,8},{8,9},{9,10},{10,1... | collective-permute-start | bytes 1544 | tf_op jit(solution)/shard_map/ppermute | solution.py:34
  83.3 2.0 %collective-permute-start.1 = (bf16[4,64]{0,1:T(8,128)(2,1)S(1)}, bf16[4,64]{0,1:T(8,128)(2,1)S(1)}, u32[]{:S(2)}, u32[]{:S(2)}) collective-permute-start(bf16[4,64]{0,1:T(8,128)(2,1)S(1)} %get-tuple-element.10), channel_id=1, source_target_pairs={{1,0},{2,1},{3,2},{4,3},{5,4},{6,5},{7,6},{8,7},{9,8},{10,9},{11,1... | collective-permute-start | bytes 1544 | tf_op jit(solution)/shard_map/ppermute | solution.py:35
  85.3 3.0 %collective-permute-done.1 = bf16[4,64]{0,1:T(8,128)(2,1)S(1)} collective-permute-done((bf16[4,64]{0,1:T(8,128)(2,1)S(1)}, bf16[4,64]{0,1:T(8,128)(2,1)S(1)}, u32[]{:S(2)}, u32[]{:S(2)}) %collective-permute-start.1) | collective-permute-done | bytes 544 | tf_op jit(solution)/shard_map/ppermute | solution.py:35
  88.4 0.7 broadcast_in_dim.60
  89.1 4.2 %all-to-all-start.2 = ((bf16[4,264,64]{1,2,0:T(8,128)(2,1)}), bf16[4,264,64]{1,2,0:T(8,128)(2,1)S(1)}, u32[]{:S(2)}, u32[]{:S(2)}) async-start(bf16[4,264,64]{1,2,0:T(8,128)(2,1)} %broadcast_in_dim.60), calls=%async_computation.2 | async-start | bytes 393216 | tf_op jit(solution)/shard_map/all_to_all | solution.py:216
  93.3 0.7 broadcast_divide_fusion
  94.0 4.5 %all-to-all-done.2 = bf16[4,264,64]{1,2,0:T(8,128)(2,1)S(1)} async-done(((bf16[4,264,64]{1,2,0:T(8,128)(2,1)}), bf16[4,264,64]{1,2,0:T(8,128)(2,1)S(1)}, u32[]{:S(2)}, u32[]{:S(2)}) %all-to-all-start.2) | async-done | bytes 135200 | tf_op jit(solution)/shard_map/all_to_all | solution.py:216
  98.6 0.1 copy.26
  98.7 0.1 copy.27
  98.8 0.1 fusion.44
  98.9 0.1 copy.24
  99.0 0.1 copy.25
  99.2 0.1 pad_maximum_fusion.main_ref
  99.3 19.4 %decode.1 = f32[4,2048,128]{2,1,0:T(8,128)} custom-call(bf16[4,128,128]{2,1,0:T(8,128)(2,1)S(1)} %pad_maximum_fusion.main_ref, f32[4,2,8,128]{3,2,1,0:T(8,128)S(1)} %maximum_convert_fusion.edge_ref, f32[1,2048]{1,0:T(1,128)S(1)} %bitcast.47, f32[1,2048]{1,0:T(1,128)S(1)} %bitcast.46, bf16[448,2048]{1,0:T(8,128)(2,1)S(1)} %bitcast.48, ...), custom_call_target="tpu_custom_call" | custom-call | flops 11000000512 | bytes 16777216 | tf_op jit(solution)/shard_map/decode/pallas_call | solution.py:125
  (20 shorter events, 0.4 us)
Async XLA Ops:
  0.0 2.5 %copy-start = (bf16[256,1536]{1,0:T(8,128)(2,1)S(1)}, bf16[256,1536]{1,0:T(8,128)(2,1)}, u32[]{:S(2)}) copy-start(bf16[256,1536]{1,0:T(8,128)(2,1)} %param.9) | copy-start | bytes 2359300
  0.0 14.2 %copy-start.4 = (f32[256,2]{0,1:T(2,128)S(1)}, f32[256,2]{0,1:T(2,128)}, u32[]{:S(2)}) copy-start(f32[256,2]{0,1:T(2,128)} %param.11) | copy-start | bytes 6148
  0.0 14.2 %copy-start.2 = (bf16[1536,64]{0,1:T(8,128)(2,1)S(1)}, bf16[1536,64]{0,1:T(8,128)(2,1)}, u32[]{:S(2)}) copy-start(bf16[1536,64]{0,1:T(8,128)(2,1)} %param.14) | copy-start | bytes 589828
  1.0 60.3 %copy-start.3 = (pred[32,256]{1,0:T(8,128)(4,1)}, pred[32,256]{1,0:T(8,128)(4,1)S(1)}, u32[]{:S(2)}) copy-start(pred[32,256]{1,0:T(8,128)(4,1)S(1)} %fusion.36) | copy-start | bytes 24580
  4.7 40.6 %all-to-all-start = ((bf16[32,24,1536]{2,1,0:T(8,128)(2,1)}), bf16[32,24,1536]{2,1,0:T(8,128)(2,1)S(1)}, u32[]{:S(2)}, u32[]{:S(2)}) async-start(bf16[32,24,1536]{2,1,0:T(8,128)(2,1)} %bitcast.6), calls=%async_computation | async-start | bytes 4718592 | tf_op jit(solution)/shard_map/all_to_all | solution.py:192
  61.3 38.0 %copy-start.1 = (bf16[7,64,2048]{2,1,0:T(8,128)(2,1)S(1)}, bf16[7,64,2048]{2,1,0:T(8,128)(2,1)}, u32[]{:S(2)}) copy-start(bf16[7,64,2048]{2,1,0:T(8,128)(2,1)} %param.15) | copy-start | bytes 5505028
  64.8 12.8 %all-to-all-start.1 = ((f32[32,1,1536]{2,1,0:T(1,128)}), f32[32,1,1536]{2,1,0:T(1,128)S(1)}, u32[]{:S(2)}, u32[]{:S(2)}) async-start(f32[32,1,1536]{2,1,0:T(1,128)} %reshape.135), calls=%async_computation.1 | async-start | bytes 393216 | tf_op jit(solution)/shard_map/all_to_all | solution.py:202
  81.0 4.3 %collective-permute-start = (bf16[4,64]{0,1:T(8,128)(2,1)S(1)}, bf16[4,64]{0,1:T(8,128)(2,1)S(1)}, u32[]{:S(2)}, u32[]{:S(2)}) collective-permute-start(bf16[4,64]{0,1:T(8,128)(2,1)S(1)} %get-tuple-element.9), channel_id=1, source_target_pairs={{0,1},{1,2},{2,3},{3,4},{4,5},{5,6},{6,7},{7,8},{8,9},{9,10},{10,1... | collective-permute-start | bytes 1544 | tf_op jit(solution)/shard_map/ppermute | solution.py:34
  83.3 5.1 %collective-permute-start.1 = (bf16[4,64]{0,1:T(8,128)(2,1)S(1)}, bf16[4,64]{0,1:T(8,128)(2,1)S(1)}, u32[]{:S(2)}, u32[]{:S(2)}) collective-permute-start(bf16[4,64]{0,1:T(8,128)(2,1)S(1)} %get-tuple-element.10), channel_id=1, source_target_pairs={{1,0},{2,1},{3,2},{4,3},{5,4},{6,5},{7,6},{8,7},{9,8},{10,9},{11,1... | collective-permute-start | bytes 1544 | tf_op jit(solution)/shard_map/ppermute | solution.py:35
  89.1 9.4 %all-to-all-start.2 = ((bf16[4,264,64]{1,2,0:T(8,128)(2,1)}), bf16[4,264,64]{1,2,0:T(8,128)(2,1)S(1)}, u32[]{:S(2)}, u32[]{:S(2)}) async-start(bf16[4,264,64]{1,2,0:T(8,128)(2,1)} %broadcast_in_dim.60), calls=%async_computation.2 | async-start | bytes 393216 | tf_op jit(solution)/shard_map/all_to_all | solution.py:216

commit v3 on v2

--- a/solution.py
+++ b/solution.py
@@ -15,6 +15,7 @@
 )
 PI_INV = 0.3183098861837907
 SEQS = 4
+SIDE = 4
 
 
 def snake(values, freq, inv_alpha):
@@ -27,17 +28,320 @@
     return values + jnp.minimum(q * t, 1.0) * inv_alpha
 
 
-def edge_rows(value, width):
-    size = lax.axis_size("expert")
-    up = [(i, (i + 1) % size) for i in range(size - 1)]
-    down = [(j, i) for i, j in up]
-    before = lax.ppermute(value[-width:], "expert", up)
-    after = lax.ppermute(value[:width], "expert", down)
-    return jnp.concatenate([before, value, after], axis=0)
+def distance(step):
+    return min(step[0], SIDE - step[0]) + min(step[1], SIDE - step[1])
+
+
+OFFSETS = [(0, 0, 0), (0, 0, 1)] + sorted(
+    [
+        (dx, dz, dc)
+        for dx in range(SIDE)
+        for dz in range(SIDE)
+        for dc in range(2)
+        if (dx, dz) != (0, 0)
+    ],
+    key=lambda step: (-distance(step), step[2]),
+)
+GROUPS = ((0, 10), (10, 20), (20, 28), (28, 32))
+PACKS = (8, 16, 24, 32)
+MESH = pl.DeviceIdType.MESH
+
+
+def gelu(v):
+    return 0.5 * v * (1.0 + jnp.tanh(0.7978845608 * (v + 0.044715 * v * v * v)))
+
+
+def expert_kernel(
+    frames_hbm, ids_hbm, gates_hbm, proj_hbm, up_hbm, down_hbm,
+    main_ref, edge_ref,
+    frames, ids, gates, proj, ranks, send, recv, rows_in, hidden, up_w, down_w, proj_w, table,
+    picks, base, answer, returned, packed, ends, main_buf, edge_buf,
+    w_sems, self_sem, out_s, out_r, back_s, back_r, main_s, main_r, end_s, end_r,
+):
+    expert = lax.axis_index("expert")
+    seg = lax.axis_index("seg")
+    x, z, core = expert // (2 * SIDE), (expert // 2) % SIDE, expert % 2
+
+    def toward(step):
+        dx, dz, dc = step
+        return (((x + dx) % SIDE) * SIDE + (z + dz) % SIDE) * 2 + (core + dc) % 2
+
+    def away(step):
+        dx, dz, dc = step
+        return (((x + SIDE - dx) % SIDE) * SIDE + (z + SIDE - dz) % SIDE) * 2 + (core + dc) % 2
+
+    count = len(OFFSETS)
+    sides = ((expert + 1) % count, (expert + count - 1) % count)
+    barrier = pltpu.get_barrier_semaphore()
+    for step in OFFSETS[1:]:
+        pl.semaphore_signal(barrier, inc=1, device_id={"expert": toward(step)}, device_id_type=MESH)
+    for ds in range(1, SEQS):
+        for to in (expert,) + sides:
+            pl.semaphore_signal(
+                barrier,
+                inc=1,
+                device_id={"seg": (seg + ds) % SEQS, "expert": to},
+                device_id_type=MESH,
+            )
+    gets = [
+        pltpu.make_async_copy(src, dst, w_sems.at[k])
+        for k, (src, dst) in enumerate(
+            [
+                (ids_hbm, ids), (frames_hbm, frames), (gates_hbm, gates), (proj_hbm, proj),
+                (up_hbm, up_w), (down_hbm, down_w),
+            ]
+        )
+    ]
+    for get in gets:
+        get.start()
+
+    tokens, dim = frames.shape
+    slots = recv.shape[1]
+    gets[0].wait()
+    name = lax.broadcasted_iota(jnp.int32, (count, tokens), 0)
+    named = (ids[0:1, :] == name) | (ids[1:2, :] == name)
+    line = lax.broadcasted_iota(jnp.int32, (tokens, tokens), 0)
+    across = lax.broadcasted_iota(jnp.int32, (tokens, tokens), 1)
+    earlier = jnp.where(line < across, 1.0, 0.0).astype(jnp.bfloat16)
+    rank = jnp.dot(
+        jnp.where(named, 1.0, 0.0).astype(jnp.bfloat16), earlier, preferred_element_type=jnp.float32
+    )
+    ranks[...] = jnp.where(named, rank, -1.0)
+    gets[1].wait()
+    slot = lax.broadcasted_iota(jnp.int32, (slots, 1), 0).astype(jnp.float32)
+
+    def pack(lo, hi):
+        rows = [
+            jnp.where(ranks[pl.ds(toward(OFFSETS[i]), 1), :] == slot, 1.0, 0.0) for i in range(lo, hi)
+        ]
+        chosen = jnp.concatenate(rows, axis=0).astype(jnp.bfloat16)
+        for n in range(dim // 512):
+            lanes = slice(512 * n, 512 * n + 512)
+            value = jnp.dot(chosen, frames[:, lanes], preferred_element_type=jnp.float32)
+            send[lo:hi, :, lanes] = value.astype(jnp.bfloat16).reshape(hi - lo, slots, 512)
+
+    outs = [None] * count
+
+    def dispatch(lo, hi):
+        for i in range(lo, hi):
+            if i == 0:
+                outs[i] = pltpu.make_async_copy(send.at[0], recv.at[0], self_sem)
+            else:
+                outs[i] = pltpu.make_async_remote_copy(
+                    src_ref=send.at[i],
+                    dst_ref=recv.at[i],
+                    send_sem=out_s.at[i],
+                    recv_sem=out_r.at[i],
+                    device_id={"expert": toward(OFFSETS[i])},
+                    device_id_type=MESH,
+                )
+            outs[i].start()
+
+    pack(0, PACKS[0])
+    pl.semaphore_wait(barrier, count - 1 + 3 * (SEQS - 1))
+    start = 0
+    for lo, hi in zip(PACKS, PACKS[1:]):
+        dispatch(start, lo)
+        pack(lo, hi)
+        start = lo
+    dispatch(start, count)
+
+    gets[2].wait()
+    gets[3].wait()
+    lat = proj.shape[0]
+    proj_w[0:lat, :] = proj[...]
+    proj_w[lat : 2 * lat, :] = proj[...]
+    base[...] = lax.dot_general(
+        frames[...], proj_w[...], (((1,), (1,)), ((), ())), preferred_element_type=jnp.float32
+    )
+    table[...] = jnp.zeros_like(table)
+    table[0:2, :] = ids[...].astype(jnp.float32)
+    table[8:10, :] = gates[...]
+    turned = jnp.transpose(table[...])
+    choice = [turned[:, 0:1], turned[:, 1:2]]
+    gate = [turned[:, 8:9], turned[:, 9:10]]
+    lane = lax.broadcasted_iota(jnp.int32, (tokens, 128), 1).astype(jnp.float32)
+    hits = [lane == choice[0], lane == choice[1]]
+    named = jnp.where(hits[0] | hits[1], 1.0, 0.0).astype(jnp.bfloat16)
+    before = jnp.where(across < line, 1.0, 0.0).astype(jnp.bfloat16)
+    rank = jnp.dot(before, named, preferred_element_type=jnp.float32)
+    spot = lax.broadcasted_iota(jnp.int32, (tokens, count * slots), 1).astype(jnp.float32)
+    for c in range(2):
+        dest = choice[c] * slots + jnp.sum(
+            jnp.where(hits[c], rank, 0.0), axis=1, keepdims=True
+        )
+        picks[pl.ds(c * tokens, tokens), :] = jnp.where(spot == dest, 1.0, 0.0).astype(jnp.bfloat16)
+
+    gets[4].wait()
+    gets[5].wait()
+    backs = [None] * count
+    first = lax.broadcasted_iota(jnp.int32, (1, 2 * lat), 1) < lat
+    width = 512
+    for lo, hi in GROUPS:
+        for i in range(lo, hi):
+            if i == 0:
+                outs[i].wait()
+            else:
+                outs[i].wait_recv()
+        size = (hi - lo) * slots
+        rows_in[0:size, :] = recv[lo:hi].reshape(size, recv.shape[2])
+
+        @pl.loop(0, hidden.shape[1] // width)
+        def _(n):
+            lanes = pl.ds(pl.multiple_of(n * width, width), width)
+            value = jnp.dot(
+                rows_in[0:size, :], up_w[0, :, lanes], preferred_element_type=jnp.float32
+            )
+            hidden[0:size, lanes] = gelu(value).astype(jnp.bfloat16)
+
+        sent = jnp.zeros((size, 2 * lat), jnp.float32)
+        for n in range(rows_in.shape[1] // width):
+            lanes = slice(n * width, n * width + width)
+            value = jnp.dot(
+                hidden[0:size, :], down_w[0, :, lanes], preferred_element_type=jnp.float32
+            ).astype(jnp.bfloat16)
+            sent = sent + lax.dot_general(
+                value, proj_w[:, lanes], (((1,), (1,)), ((), ())), preferred_element_type=jnp.float32
+            )
+        high = sent.astype(jnp.bfloat16).astype(jnp.float32)
+        split = jnp.where(first, high, sent - high).astype(jnp.bfloat16)
+        answer[lo:hi] = split.reshape(hi - lo, slots, 2 * lat)
+        for i in range(lo, hi):
+            if i == 0:
+                backs[i] = pltpu.make_async_copy(answer.at[i], returned.at[expert], back_r.at[i])
+            else:
+                backs[i] = pltpu.make_async_remote_copy(
+                    src_ref=answer.at[i],
+                    dst_ref=returned.at[expert],
+                    send_sem=back_s.at[i],
+                    recv_sem=back_r.at[i],
+                    device_id={"expert": away(OFFSETS[i])},
+                    device_id_type=MESH,
+                )
+            backs[i].start()
+
+    for i in range(count):
+        if i == 0:
+            backs[i].wait()
+        else:
+            pltpu.make_async_remote_copy(
+                src_ref=answer.at[i],
+                dst_ref=returned.at[toward(OFFSETS[i])],
+                send_sem=back_s.at[i],
+                recv_sem=back_r.at[i],
+                device_id={"expert": away(OFFSETS[i])},
+                device_id_type=MESH,
+            ).wait_recv()
+    got = jnp.dot(
+        picks[...],
+        returned[...].reshape(count * slots, 2 * lat),
+        preferred_element_type=jnp.float32,
+    )
+    got = got + pltpu.roll(got, lat, axis=1)
+    latent = base[...] + gate[0] * got[0:tokens] + gate[1] * got[tokens:]
+    latent = latent.astype(jnp.bfloat16).astype(jnp.float32)
+    half = tokens // 2
+    packed[...] = jnp.where(first, latent[0:half], latent[half:]).astype(jnp.bfloat16)
+    ends[0] = latent[tokens - 8 :]
+    ends[1] = latent[0:8]
+
+    sends = []
+    for side in range(2):
+        for ds in range(SEQS):
+            k = side * SEQS + ds
+            copy = pltpu.make_async_remote_copy(
+                src_ref=ends.at[side],
+                dst_ref=edge_buf.at[seg, side],
+                send_sem=end_s.at[k],
+                recv_sem=end_r.at[k],
+                device_id={"seg": (seg + ds) % SEQS, "expert": sides[side]},
+                device_id_type=MESH,
+            )
+            copy.start()
+            sends.append((copy, edge_buf.at[(seg + SEQS - ds) % SEQS, side], end_s.at[k], end_r.at[k]))
+    for ds in range(1, SEQS):
+        copy = pltpu.make_async_remote_copy(
+            src_ref=packed,
+            dst_ref=main_buf.at[seg],
+            send_sem=main_s.at[ds],
+            recv_sem=main_r.at[ds],
+            device_id={"seg": (seg + ds) % SEQS, "expert": expert},
+            device_id_type=MESH,
+        )
+        copy.start()
+        sends.append((copy, main_buf.at[(seg + SEQS - ds) % SEQS], main_s.at[ds], main_r.at[ds]))
+    main_buf[seg] = packed[...]
+    for k, (copy, landing, ss, rs) in enumerate(sends):
+        pltpu.make_async_remote_copy(
+            src_ref=ends.at[0] if k < 2 * SEQS else packed,
+            dst_ref=landing,
+            send_sem=ss,
+            recv_sem=rs,
+            device_id={"seg": (seg + 1) % SEQS, "expert": expert},
+            device_id_type=MESH,
+        ).wait_recv()
+    main_ref[...] = main_buf[...]
+    edge_ref[...] = edge_buf[...]
+    for copy in outs[1:] + backs[1:] + [entry[0] for entry in sends]:
+        copy.wait_send()
+
+
+def experts(frames, ids, gates, proj, up_weight, down_weight):
+    tokens, dim = frames.shape
+    count = len(OFFSETS)
+    slots = 3 * tokens // count
+    hid = up_weight.shape[2]
+    lat = proj.shape[0]
+    vmem = pl.BlockSpec(memory_space=pltpu.VMEM)
+    anywhere = pl.BlockSpec(memory_space=pltpu.HBM)
+    bf16, f32 = jnp.bfloat16, jnp.float32
+    top = max(hi - lo for lo, hi in GROUPS) * slots
+    sems = lambda *shape: pltpu.SemaphoreType.DMA(shape)
+    return pl.pallas_call(
+        expert_kernel,
+        out_shape=(
+            jax.ShapeDtypeStruct((SEQS, tokens // 2, 2 * lat), bf16),
+            jax.ShapeDtypeStruct((SEQS, 2, 8, 2 * lat), f32),
+        ),
+        in_specs=[anywhere] * 6,
+        out_specs=(vmem, vmem),
+        scratch_shapes=[
+            pltpu.VMEM(frames.shape, bf16),
+            pltpu.VMEM(ids.shape, jnp.int32),
+            pltpu.VMEM(gates.shape, f32),
+            pltpu.VMEM(proj.shape, bf16),
+            pltpu.VMEM((count, tokens), f32),
+            pltpu.VMEM((count, slots, dim), bf16),
+            pltpu.VMEM((count, slots, dim), bf16),
+            pltpu.VMEM((top, dim), bf16),
+            pltpu.VMEM((top, hid), bf16),
+            pltpu.VMEM(up_weight.shape, bf16),
+            pltpu.VMEM(down_weight.shape, bf16),
+            pltpu.VMEM((2 * lat, dim), bf16),
+            pltpu.VMEM((128, tokens), f32),
+            pltpu.VMEM((2 * tokens, count * slots), bf16),
+            pltpu.VMEM((tokens, 2 * lat), f32),
+            pltpu.VMEM((count, slots, 2 * lat), bf16),
+            pltpu.VMEM((count, slots, 2 * lat), bf16),
+            pltpu.VMEM((tokens // 2, 2 * lat), bf16),
+            pltpu.VMEM((2, 8, 2 * lat), f32),
+            pltpu.VMEM((SEQS, tokens // 2, 2 * lat), bf16),
+            pltpu.VMEM((SEQS, 2, 8, 2 * lat), f32),
+            sems(6), sems(), sems(count), sems(count), sems(count), sems(count),
+            sems(SEQS), sems(SEQS), sems(2 * SEQS), sems(2 * SEQS),
+        ],
+        compiler_params=pltpu.CompilerParams(
+            collective_id=0, has_side_effects=True, vmem_limit_bytes=63 << 20
+        ),
+        cost_estimate=pl.CostEstimate(
+            flops=10 * 10**9, bytes_accessed=16 << 20, transcendentals=0
+        ),
+        name="experts",
+    )(frames, ids, gates, proj, up_weight, down_weight)
 
 
 def decode_kernel(
-    main_ref, edge_ref, freq_ref, inv_ref, conv_hbm, up_hbm, out_hbm,
+    main_ref, edge_ref, alpha_ref, conv_hbm, up_hbm, out_hbm,
     plain, pairs, cols, rims, wide, act, here, other, tile, conv_w, up_w, in_sems, out_sems,
 ):
     rows = main_ref.shape[1] * 2
@@ -73,8 +377,9 @@
     @pl.loop(0, act.shape[1] // 256)
     def _(n):
         lanes = pl.ds(pl.multiple_of(n * 256, 256), 256)
-        freq = freq_ref[:, lanes]
-        inv = inv_ref[:, lanes]
+        alpha = alpha_ref[:, lanes]
+        freq = alpha * PI_INV
+        inv = 1.0 / alpha
         weight = conv_w[:, lanes]
         for part, size in [(s * rows, rows) for s in range(SEQS)] + [(total, 16)]:
             value = jnp.dot(
@@ -121,11 +426,11 @@
     rows = main.shape[1] * 2
     total = SEQS * rows + 16
     vmem = pl.BlockSpec(memory_space=pltpu.VMEM)
-    anywhere = pl.BlockSpec(memory_space=pl.ANY)
+    anywhere = pl.BlockSpec(memory_space=pltpu.HBM)
     return pl.pallas_call(
         decode_kernel,
         out_shape=jax.ShapeDtypeStruct((SEQS, rows * 8, first_up.shape[2]), jnp.float32),
-        in_specs=[vmem, vmem, vmem, vmem, anywhere, anywhere],
+        in_specs=[vmem, vmem, vmem, anywhere, anywhere],
         out_specs=anywhere,
         scratch_shapes=[
             pltpu.VMEM((rows + 24, 128), jnp.float32),
@@ -142,14 +447,13 @@
             pltpu.SemaphoreType.DMA((2,)),
             pltpu.SemaphoreType.DMA((SEQS,)),
         ],
-        compiler_params=pltpu.CompilerParams(vmem_limit_bytes=48 << 20),
+        compiler_params=pltpu.CompilerParams(vmem_limit_bytes=63 << 20),
         cost_estimate=pl.CostEstimate(flops=11 * 10**9, bytes_accessed=16 << 20, transcendentals=0),
         name="decode",
     )(
         main,
         edges,
-        (snake_first * PI_INV)[None, :],
-        (1.0 / snake_first)[None, :],
+        snake_first[None, :],
         in_conv.reshape(-1, channels),
         first_up,
     )
@@ -166,59 +470,9 @@
     snake_first,
     first_up,
 ):
-    tok_rows, model_dim = frames.shape
-    num_experts = lax.axis_size("expert")
-    capacity = 3 * tok_rows // num_experts
-    lat_dim = out_weight.shape[1]
-
-    experts = jnp.arange(num_experts, dtype=jnp.int32)[:, None]
-    first = expert_ids[:, 0][None, :] == experts
-    second = expert_ids[:, 1][None, :] == experts
-    named = first | second
-    row = jnp.arange(tok_rows, dtype=jnp.int32)
-    earlier = (row[:, None] < row[None, :]).astype(jnp.bfloat16)
-    rank = jnp.dot(named.astype(jnp.bfloat16), earlier, preferred_element_type=jnp.float32)
-    slots = jnp.arange(capacity, dtype=jnp.int32).astype(jnp.float32)
-    pick = (rank[:, None, :] == slots[None, :, None]) & named[:, None, :]
-    gates = jnp.where(first, gate_weights[:, 0][None, :], 0.0) + jnp.where(
-        second, gate_weights[:, 1][None, :], 0.0
-    )
-    weighted = jnp.where(pick, gates[:, None, :], 0.0).reshape(-1, tok_rows)
-
-    send = jnp.dot(
-        pick.reshape(-1, tok_rows).astype(jnp.bfloat16), frames, preferred_element_type=jnp.float32
-    ).astype(jnp.bfloat16)
-    send = send.reshape(num_experts, capacity, model_dim)
-    received = lax.all_to_all(send, "expert", split_axis=0, concat_axis=0, tiled=True)
-    flat_rows = received.reshape(-1, model_dim)
-    hidden_units = jax.nn.gelu(
-        jnp.dot(flat_rows, up_weight[0], preferred_element_type=jnp.float32), approximate=True
-    ).astype(jnp.bfloat16)
-    expert_out = jnp.dot(hidden_units, down_weight[0], preferred_element_type=jnp.float32).astype(
-        jnp.bfloat16
-    )
-    projected = jnp.dot(expert_out, out_weight, preferred_element_type=jnp.float32)
-    projected = projected.reshape(num_experts, capacity, lat_dim)
-    returned = lax.all_to_all(projected, "expert", split_axis=0, concat_axis=0, tiled=True)
-    gated = lax.dot_general(
-        weighted,
-        returned.reshape(-1, lat_dim),
-        (((0,), (0,)), ((), ())),
-        precision=lax.Precision.HIGHEST,
-        preferred_element_type=jnp.float32,
-    )
-    latent = jnp.dot(frames, out_weight, preferred_element_type=jnp.float32) + gated
-    latent_low = latent.astype(jnp.bfloat16)
-
-    padded = edge_rows(latent_low, 4)
-    num_seg = lax.axis_size("seg")
-    spread = jnp.broadcast_to(padded[None], (num_seg,) + padded.shape)
-    sequences = lax.all_to_all(spread, "seg", split_axis=0, concat_axis=0, tiled=True)
-    half = tok_rows // 2
-    main = jnp.concatenate([sequences[:, 4 : 4 + half], sequences[:, 4 + half : 4 + tok_rows]], axis=2)
-    left = jnp.pad(sequences[:, 0:4], ((0, 0), (4, 0), (0, 64)))
-    right = jnp.pad(sequences[:, 4 + tok_rows :], ((0, 0), (0, 4), (0, 64)))
-    edges = jnp.stack([left, right], axis=1).astype(jnp.float32)
+    main, edges = experts(
+        frames, expert_ids.T, gate_weights.T, out_weight.T, up_weight, down_weight
+    )
     return decode(main, edges, in_conv, snake_first, first_up)
 
 

time: 120 us -> 79.1 us (0.66)
  Pallas kernels: 19.4 us -> 78.8 us
  waiting for transfers between devices: 46.7 us -> 0 us
  matrix products: 22.8 us -> 0 us
  starting transfers between devices: 22.3 us -> 0 us
  local copies, waits for them, and re-layouts: 4.58 us -> 0 us
  other arithmetic: 2.83 us -> 0 us
    pallas_call x0 -> x1, Pallas kernels: none -> 57.4 us  [experts(): pl.pallas_call(expert_kernel, out_shape=(jax.ShapeDtypeStruct((SEQS, toke...]
    all_to_all x3 -> x0, waiting for transfers between devices: 43.6 us -> none  [the longest x1 30.8 us: local(): lax.all_to_all(send, 'expert', split_axis=0, concat_axis=0, tiled=True)]
    dot_general x6 -> x0, matrix products: 22.8 us -> none  [the longest x1 16 us: local(): jnp.dot(hidden_units, down_weight[0], preferred_element_type=jnp.float32)]
    all_to_all x3 -> x0, starting transfers between devices: 18 us -> none  [the longest x1 9.42 us: local(): lax.all_to_all(send, 'expert', split_axis=0, concat_axis=0, tiled=True)]
    ppermute x2 -> x0, starting transfers between devices: 4.31 us -> none  [the longest x1 2.29 us: edge_rows(): before = lax.ppermute(value[-width:], 'expert', up)]
    ppermute x2 -> x0, waiting for transfers between devices: 3.01 us -> none  [the longest x1 3.01 us: edge_rows(): after = lax.ppermute(value[:width], 'expert', down)]
    pallas_call x1, Pallas kernels: 19.4 us -> 21.4 us  [decode(): pl.pallas_call(decode_kernel, out_shape=jax.ShapeDtypeStruct((SEQS, rows...]
    unnamed x16 -> x0, local copies, waits for them, and re-layouts: 1.54 us -> none
  transfers between devices with their start and end apart: 5 -> 0, of which waited for: 4 -> 0; matrix products, arithmetic and copies ran while one was open for 1% -> 0% of each run, Pallas kernels for 0% -> 0%
where the time goes in v3:
time: 79.1 us; the launch traced here: 78.9 us
  Pallas kernels  78.8 us (100%)
    pallas_call x1, Pallas kernels, experts(): pl.pallas_call(expert_kernel, out_shape=(jax.ShapeDtypeStruct((SEQS, toke...  57.4 us
    pallas_call x1, Pallas kernels, decode(): pl.pallas_call(decode_kernel, out_shape=jax.ShapeDtypeStruct((SEQS, rows...  21.4 us

profile of v3, /device:TPU:1, one launch (start us, length us, event | category | flops | bytes accessed | tf_op | source)
XLA Modules:
  0.0 78.9 jit_solution(5791971714657741425)
XLA Ops:
  0.0 57.4 %experts.1 = (bf16[4,128,128]{2,1,0:T(8,128)(2,1)}, f32[4,2,8,128]{3,2,1,0:T(8,128)}) custom-call(bf16[256,1536]{1,0:T(8,128)(2,1)} %frames_hbm.1, s32[2,256]{1,0:T(2,128)} %bitcast.8, f32[2,256]{1,0:T(2,128)} %bitcast.9, bf16[64,1536]{1,0:T(8,128)(2,1)} %bitcast.6, bf16[1,1536,2048]{2,1,0:T(8,128)(2,1)} %up_hbm.2, bf16[1,2048,1536]{2,1,0:T(8,128)(2,1)} %down_hbm.1), custom_call_target="tpu_custom_call" | custom-call | flops 10000000000 | bytes 16777216 | tf_op jit(solution)/shard_map/experts/pallas_call | solution.py:300
  57.4 21.4 %decode.1 = f32[4,2048,128]{2,1,0:T(8,128)} custom-call(bf16[4,128,128]{2,1,0:T(8,128)(2,1)} %get-tuple-element.7.main_ref, f32[4,2,8,128]{3,2,1,0:T(8,128)} %get-tuple-element.8.edge_ref, f32[1,2048]{1,0:T(1,128)} %bitcast.7, bf16[448,2048]{1,0:T(8,128)(2,1)} %bitcast.5, bf16[16,2048,128]{2,1,0:T(8,128)(2,1)} %up_hbm.3), custom_call_target="tpu_custom_call" | custom-call | flops 11000000512 | bytes 16777216 | tf_op jit(solution)/shard_map/decode/pallas_call | solution.py:430

commit v4 on v3

--- a/solution.py
+++ b/solution.py
@@ -28,22 +28,14 @@
     return values + jnp.minimum(q * t, 1.0) * inv_alpha
 
 
-def distance(step):
-    return min(step[0], SIDE - step[0]) + min(step[1], SIDE - step[1])
-
-
-OFFSETS = [(0, 0, 0), (0, 0, 1)] + sorted(
-    [
-        (dx, dz, dc)
-        for dx in range(SIDE)
-        for dz in range(SIDE)
-        for dc in range(2)
-        if (dx, dz) != (0, 0)
-    ],
-    key=lambda step: (-distance(step), step[2]),
-)
-GROUPS = ((0, 10), (10, 20), (20, 28), (28, 32))
-PACKS = (8, 16, 24, 32)
+OFFSETS = [
+    (dx, (dx - shift) % SIDE, dc)
+    for shift in (0, 1, 3, 2)
+    for dc in range(2)
+    for dx in range(SIDE)
+]
+WAVE = 8
+WAVES = tuple((lo, lo + WAVE) for lo in range(0, len(OFFSETS), WAVE))
 MESH = pl.DeviceIdType.MESH
 
 
@@ -137,14 +129,13 @@
                 )
             outs[i].start()
 
-    pack(0, PACKS[0])
+    pack(*WAVES[0])
     pl.semaphore_wait(barrier, count - 1 + 3 * (SEQS - 1))
-    start = 0
-    for lo, hi in zip(PACKS, PACKS[1:]):
-        dispatch(start, lo)
-        pack(lo, hi)
-        start = lo
-    dispatch(start, count)
+    dispatch(*WAVES[0])
+    pack(*WAVES[1])
+    dispatch(*WAVES[1])
+    for wave in WAVES[2:]:
+        pack(*wave)
 
     gets[2].wait()
     gets[3].wait()
@@ -177,12 +168,14 @@
     backs = [None] * count
     first = lax.broadcasted_iota(jnp.int32, (1, 2 * lat), 1) < lat
     width = 512
-    for lo, hi in GROUPS:
+    for turn, (lo, hi) in enumerate(WAVES):
         for i in range(lo, hi):
             if i == 0:
                 outs[i].wait()
             else:
                 outs[i].wait_recv()
+        if turn + 2 < len(WAVES):
+            dispatch(*WAVES[turn + 2])
         size = (hi - lo) * slots
         rows_in[0:size, :] = recv[lo:hi].reshape(size, recv.shape[2])
 
@@ -295,7 +288,7 @@
     vmem = pl.BlockSpec(memory_space=pltpu.VMEM)
     anywhere = pl.BlockSpec(memory_space=pltpu.HBM)
     bf16, f32 = jnp.bfloat16, jnp.float32
-    top = max(hi - lo for lo, hi in GROUPS) * slots
+    top = WAVE * slots
     sems = lambda *shape: pltpu.SemaphoreType.DMA(shape)
     return pl.pallas_call(
         expert_kernel,
@@ -340,12 +333,11 @@
     )(frames, ids, gates, proj, up_weight, down_weight)
 
 
-def decode_kernel(
-    main_ref, edge_ref, alpha_ref, conv_hbm, up_hbm, out_hbm,
-    plain, pairs, cols, rims, wide, act, here, other, tile, conv_w, up_w, in_sems, out_sems,
-):
+def decode_kernel(main_ref, edge_ref, alpha_ref, conv_hbm, up_hbm, out_hbm, *scratch):
+    plain, pairs, shifted, tile, conv_w, up_w, in_sems, out_sems = scratch[:8]
+    cols, act = scratch[8 : 8 + SEQS], scratch[8 + SEQS :]
     rows = main_ref.shape[1] * 2
-    total = SEQS * rows
+    height = rows + 16
     get_conv = pltpu.make_async_copy(conv_hbm, conv_w.at[pl.ds(0, 448)], in_sems.at[0])
     get_conv.start()
     get_up = pltpu.make_async_copy(up_hbm, up_w, in_sems.at[1])
@@ -355,68 +347,55 @@
     keep_right = jnp.where(slab == lax.axis_size("expert") - 1, 0.0, 1.0)
     conv_w[pl.ds(448, 64), :] = jnp.zeros((64, conv_w.shape[1]), jnp.bfloat16)
     plain[...] = jnp.zeros_like(plain)
-    rims[...] = jnp.zeros_like(rims)
+
     for s in range(SEQS):
         body = main_ref[s].astype(jnp.float32)
         half = rows // 2
-        plain[pl.ds(8, half), 0:64] = body[:, 0:64]
-        plain[pl.ds(8 + half, half), 0:64] = body[:, 64:128]
-        plain[pl.ds(0, 8), 0:64] = edge_ref[s, 0][:, 0:64] * keep_left
-        plain[pl.ds(8 + rows, 8), 0:64] = edge_ref[s, 1][:, 0:64] * keep_right
-        pairs[...] = plain[pl.ds(0, rows + 16), :] + pltpu.roll(
-            plain[pl.ds(1, rows + 16), :], 64, axis=1
+        plain[pl.ds(8, 8), 0:64] = edge_ref[s, 0][:, 0:64] * keep_left
+        plain[pl.ds(16, half), 0:64] = body[:, 0:64]
+        plain[pl.ds(16 + half, half), 0:64] = body[:, 64:128]
+        plain[pl.ds(16 + rows, 8), 0:64] = edge_ref[s, 1][:, 0:64] * keep_right
+        size = pairs.shape[0]
+        pairs[...] = plain[pl.ds(0, size), :] + pltpu.roll(plain[pl.ds(1, size), :], 64, axis=1)
+        for m in range(4):
+            cols[s][:, 128 * m : 128 * m + 128] = pairs[pl.ds(5 + 2 * m, height), :].astype(
+                jnp.bfloat16
+            )
+    get_conv.wait()
+
+    def activate(s, lanes):
+        alpha = alpha_ref[:, lanes]
+        value = jnp.dot(cols[s][...], conv_w[:, lanes], preferred_element_type=jnp.float32)
+        value = snake(value, alpha * PI_INV, 1.0 / alpha)
+        value = jnp.concatenate(
+            [value[0:8] * keep_left, value[8 : 8 + rows], value[8 + rows :] * keep_right], axis=0
         )
-        for m in range(4):
-            lanes = slice(128 * m, 128 * m + 128)
-            cols[pl.ds(s * rows, rows), lanes] = pairs[pl.ds(5 + 2 * m, rows), :].astype(jnp.bfloat16)
-            rims[pl.ds(2 * s, 1), lanes] = pairs[pl.ds(4 + 2 * m, 1), :]
-            rims[pl.ds(2 * s + 1, 1), lanes] = pairs[pl.ds(5 + 2 * m + rows, 1), :]
-    cols[pl.ds(total, 16), :] = rims[...].astype(jnp.bfloat16)
-    get_conv.wait()
-
-    @pl.loop(0, act.shape[1] // 256)
+        act[s][:, lanes] = value.astype(jnp.bfloat16)
+
+    @pl.loop(0, conv_w.shape[1] // 256)
     def _(n):
-        lanes = pl.ds(pl.multiple_of(n * 256, 256), 256)
-        alpha = alpha_ref[:, lanes]
-        freq = alpha * PI_INV
-        inv = 1.0 / alpha
-        weight = conv_w[:, lanes]
-        for part, size in [(s * rows, rows) for s in range(SEQS)] + [(total, 16)]:
-            value = jnp.dot(
-                cols[pl.ds(part, size), :], weight, preferred_element_type=jnp.float32
-            )
-            act[pl.ds(part, size), lanes] = snake(value, freq, inv).astype(jnp.bfloat16)
-
-    line = lax.broadcasted_iota(jnp.int32, (16, 1), 0)
-    gone = jnp.where(line % 2 == 0, keep_left, keep_right)
-    edge_act = act[pl.ds(total, 16), :].astype(jnp.float32) * gone
-    act[pl.ds(total, 16), :] = edge_act.astype(jnp.bfloat16)
+        activate(0, pl.ds(pl.multiple_of(n * 256, 256), 256))
+
     get_up.wait()
-
-    for q in range(4):
-        r = 2 * q
-        tap = (r + 12) % 16
-        near = jnp.concatenate([up_w[r + 4], up_w[r + 5]], axis=1)
-        far = jnp.concatenate([up_w[tap], up_w[tap + 1]], axis=1)
-        rim = jnp.dot(act[pl.ds(total, 16), :], far, preferred_element_type=jnp.float32)
-        for s in range(SEQS):
-            block = act[pl.ds(s * rows, rows), :]
-            here[...] = jnp.dot(block, near, preferred_element_type=jnp.float32)
-            other[pl.ds(8, rows), :] = jnp.dot(block, far, preferred_element_type=jnp.float32)
-            if q < 2:
-                other[pl.ds(7, 1), :] = rim[2 * s : 2 * s + 1]
-                shifted = other[pl.ds(7, rows), :]
-            else:
-                other[pl.ds(8 + rows, 1), :] = rim[2 * s + 1 : 2 * s + 2]
-                shifted = other[pl.ds(9, rows), :]
-            both = here[...] + shifted
+    puts = []
+    for s in range(SEQS):
+        for q in range(4):
+            r = 2 * q
+            tap = (r + 12) % 16
+            near = jnp.concatenate([up_w[r + 4], up_w[r + 5]], axis=1)
+            far = jnp.concatenate([up_w[tap], up_w[tap + 1]], axis=1)
+            buf = shifted.at[q % 2]
+            buf[...] = jnp.dot(act[s][...], far, preferred_element_type=jnp.float32)
+            if s + 1 < SEQS:
+                activate(s + 1, slice(512 * q, 512 * q + 256))
+            both = jnp.dot(act[s][...], near, preferred_element_type=jnp.float32)[8 : 8 + rows]
+            both = both + buf[pl.ds(7 if q < 2 else 9, rows), :]
+            if s + 1 < SEQS:
+                activate(s + 1, slice(512 * q + 256, 512 * q + 512))
             tile[s, pl.ds(r, rows, stride=8), :] = both[:, 0:128]
             tile[s, pl.ds(r + 1, rows, stride=8), :] = both[:, 128:256]
-    puts = [
-        pltpu.make_async_copy(tile.at[s], out_hbm.at[s], out_sems.at[s]) for s in range(SEQS)
-    ]
-    for put in puts:
-        put.start()
+        puts.append(pltpu.make_async_copy(tile.at[s], out_hbm.at[s], out_sems.at[s]))
+        puts[s].start()
     for put in puts:
         put.wait()
 
@@ -424,7 +403,6 @@
 def decode(main, edges, in_conv, snake_first, first_up):
     channels = in_conv.shape[2]
     rows = main.shape[1] * 2
-    total = SEQS * rows + 16
     vmem = pl.BlockSpec(memory_space=pltpu.VMEM)
     anywhere = pl.BlockSpec(memory_space=pltpu.HBM)
     return pl.pallas_call(
@@ -433,30 +411,21 @@
         in_specs=[vmem, vmem, vmem, anywhere, anywhere],
         out_specs=anywhere,
         scratch_shapes=[
-            pltpu.VMEM((rows + 24, 128), jnp.float32),
-            pltpu.VMEM((rows + 16, 128), jnp.float32),
-            pltpu.VMEM((total, 512), jnp.bfloat16),
-            pltpu.VMEM((16, 512), jnp.float32),
-            pltpu.VMEM((8, 128), jnp.float32),
-            pltpu.VMEM((total, channels), jnp.bfloat16),
-            pltpu.VMEM((rows, 256), jnp.float32),
-            pltpu.VMEM((rows + 16, 256), jnp.float32),
+            pltpu.VMEM((rows + 48, 128), jnp.float32),
+            pltpu.VMEM((rows + 32, 128), jnp.float32),
+            pltpu.VMEM((2, rows + 16, 256), jnp.float32),
             pltpu.VMEM((SEQS, rows * 8, first_up.shape[2]), jnp.float32),
             pltpu.VMEM((512, channels), jnp.bfloat16),
             pltpu.VMEM(first_up.shape, jnp.bfloat16),
             pltpu.SemaphoreType.DMA((2,)),
             pltpu.SemaphoreType.DMA((SEQS,)),
-        ],
+        ]
+        + [pltpu.VMEM((rows + 16, 512), jnp.bfloat16)] * SEQS
+        + [pltpu.VMEM((rows + 16, channels), jnp.bfloat16)] * SEQS,
         compiler_params=pltpu.CompilerParams(vmem_limit_bytes=63 << 20),
         cost_estimate=pl.CostEstimate(flops=11 * 10**9, bytes_accessed=16 << 20, transcendentals=0),
         name="decode",
-    )(
-        main,
-        edges,
-        snake_first[None, :],
-        in_conv.reshape(-1, channels),
-        first_up,
-    )
+    )(main, edges, snake_first[None, :], in_conv.reshape(-1, channels), first_up)
 
 
 def local(

time: 79.1 us -> 75.5 us (0.954)
  Pallas kernels: 78.8 us -> 75.1 us
    pallas_call x1, Pallas kernels: 21.4 us -> 18.3 us  [decode(): pl.pallas_call(decode_kernel, out_shape=jax.ShapeDtypeStruct((SEQS, rows...]
where the time goes in v4:
time: 75.5 us; the launch traced here: 75.2 us
  Pallas kernels  75.1 us (99%)
    pallas_call x1, Pallas kernels, experts(): pl.pallas_call(expert_kernel, out_shape=(jax.ShapeDtypeStruct((SEQS, toke...  56.8 us
    pallas_call x1, Pallas kernels, decode(): pl.pallas_call(decode_kernel, out_shape=jax.ShapeDtypeStruct((SEQS, rows...  18.3 us

profile of v4, /device:TPU:1, one launch (start us, length us, event | category | flops | bytes accessed | tf_op | source)
XLA Modules:
  0.0 75.2 jit_solution(1891633898953759121)
XLA Ops:
  0.0 56.8 %experts.1 = (bf16[4,128,128]{2,1,0:T(8,128)(2,1)}, f32[4,2,8,128]{3,2,1,0:T(8,128)}) custom-call(bf16[256,1536]{1,0:T(8,128)(2,1)} %frames_hbm.1, s32[2,256]{1,0:T(2,128)} %bitcast.8, f32[2,256]{1,0:T(2,128)} %bitcast.9, bf16[64,1536]{1,0:T(8,128)(2,1)} %bitcast.6, bf16[1,1536,2048]{2,1,0:T(8,128)(2,1)} %up_hbm.2, bf16[1,2048,1536]{2,1,0:T(8,128)(2,1)} %down_hbm.1), custom_call_target="tpu_custom_call" | custom-call | flops 10000000000 | bytes 16777216 | tf_op jit(solution)/shard_map/experts/pallas_call | solution.py:293
  56.8 18.3 %decode.1 = f32[4,2048,128]{2,1,0:T(8,128)} custom-call(bf16[4,128,128]{2,1,0:T(8,128)(2,1)} %get-tuple-element.7.main_ref, f32[4,2,8,128]{3,2,1,0:T(8,128)} %get-tuple-element.8.edge_ref, f32[1,2048]{1,0:T(1,128)} %bitcast.7, bf16[448,2048]{1,0:T(8,128)(2,1)} %bitcast.5, bf16[16,2048,128]{2,1,0:T(8,128)(2,1)} %up_hbm.3), custom_call_target="tpu_custom_call" | custom-call | flops 11000000512 | bytes 16777216 | tf_op jit(solution)/shard_map/decode/pallas_call | solution.py:408
